TPU v7x, 256 devices: a whole 4x4x8 slice. The times are simulated.
256 devices in a mesh: lat: 16 (over y_lo, z), lon: 8 (over x, y_hi), comp: 2 (over core).
Axes of the slice: x: 4, y: 4 (y_hi: 2, y_lo: 2; y = y_hi * 2 + y_lo), z: 8, core: 2. Of those that a mesh axis runs over, the one named last changes fastest.
Arguments:
- atm_state: bfloat16 [2, 32, 2048, 384], P(None, 'lat', ('lon', 'comp')), may hold values from -6 to 6
- ocean_prev: bfloat16 [2, 32, 2048, 128], P(None, 'lat', ('lon', 'comp')), may hold values from -6 to 6
- land_sea: int32 [32, 2048], P('lat', ('lon', 'comp')), may hold values 0 or 1
- window_ids: int32 [32, 2048], P('lat', ('lon', 'comp')), may hold values from 0 to 2047, as said below
- conv_atm: float32 [2, 3, 3, 384], replicated, may hold values from -2 to 2
- attn_gain: float32 [2, 384], replicated, may hold values from 0.5 to 2
- qkv_matrix: bfloat16 [2, 384, 1152], replicated, may hold values from -0.3125 to 0.3125
- attn_scales: float32 [2, 6], replicated, may hold values from 4 to 32
- out_matrix: bfloat16 [2, 384, 384], replicated, may hold values from -0.3125 to 0.3125
- mlp_gain: float32 [2, 384], replicated, may hold values from 0.5 to 2
- member_in: float32 [2, 2, 384], replicated, may hold values from 0.5 to 2
- member_out: float32 [2, 2, 1536], replicated, may hold values from 0.5 to 2
- up_matrix: bfloat16 [2, 384, 1536], replicated, may hold values from -0.3125 to 0.3125
- down_matrix: bfloat16 [2, 1536, 384], replicated, may hold values from -0.15625 to 0.15625
- flux_matrix: bfloat16 [384, 128], replicated, may hold values from -0.3125 to 0.3125
- conv_ocean: float32 [3, 3, 3, 128], replicated, may hold values from -2 to 2
- point_matrix: bfloat16 [3, 128, 128], replicated, may hold values from -0.5 to 0.5
- ocean_gain: float32 [128], replicated, may hold values from 0.5 to 2
- ocean_qkv: bfloat16 [128, 384], replicated, may hold values from -0.5 to 0.5
- ocean_scale: float32 [2], replicated, may hold values from 4 to 32
- ocean_out: bfloat16 [128, 128], replicated, may hold values from -0.5 to 0.5
- seaside_return_matrix: bfloat16 [128, 384], replicated, may hold values from -0.5 to 0.5
Outputs:
- updated_airflow_field: bfloat16 [2, 32, 2048, 384], P(None, 'lat', ('lon', 'comp'))
- updated_seaside_channels: bfloat16 [2, 32, 2048, 128], P(None, 'lat', ('lon', 'comp'))
Inputs may be any that keep to these rules, and one draw needn't show every extreme that they name: `land_sea`: 1 marks a sea column, 0 land. `window_ids`: along each latitude the value is the longitude of the first column of that column's window; it never falls along a row, every window lies inside an aligned run of 128 longitudes, and the last longitude of every row is a window of its own.
All inputs are finite; a program needn't handle non-finite values. No bound on the sum of `land_sea` on one device may be relied on, other than what follows from the above.
Results may differ from a plain program's by a relative error of at most 0.018.
Values may be sent and summed in bfloat16 or wider, within the bound.
No kernel may reach another device: no remote copies, remote signals or barrier semaphores. Data moves between devices by JAX's collectives and lax.ppermute only.
A program may use at most 64 MiB of HBM per device.

v0:
```python
import jax
import jax.numpy as jnp
from jax import lax
from jax.experimental import pallas as pl
from jax.experimental.pallas import tpu as pltpu
from jax.sharding import PartitionSpec as P


WIDTH = 384
HEADS = 6
HIDDEN = 1536
OCEAN = 128
COLS = 128
NORM_EPS = 1e-05
UNIT_EPS = 1e-06
LOG2E = 1.4426950408889634
STEP = 768
GROUP = 4
F32 = jnp.float32
BF16 = jnp.bfloat16
VM = pl.BlockSpec(memory_space=pltpu.VMEM)
SM = pl.BlockSpec(memory_space=pltpu.SMEM)
ANY = pl.BlockSpec(memory_space=pl.ANY)
PARAMS = pltpu.CompilerParams(vmem_limit_bytes=20 * 1024 * 1024)


def near(*arrays):
    return tuple(pltpu.with_memory_space_constraint(a, pltpu.VMEM) for a in arrays)


def dot(a, b):
    return jnp.dot(a, b, preferred_element_type=F32)


def dot_t(a, b):
    return lax.dot_general(a, b, (((1,), (1,)), ((), ())), preferred_element_type=F32)


def gelu(v):
    half = v * 0.5
    return half + half * lax.erf(v * 0.7071067811865476)


def norm_rows(x, gain):
    centred = x - jnp.mean(x, axis=-1, keepdims=True)
    spread = jnp.mean(centred * centred, axis=-1, keepdims=True)
    return centred * lax.rsqrt(spread + NORM_EPS) * gain


def head_mean(size):
    row = lax.broadcasted_iota(jnp.int32, (size, size), 0) // 64
    col = lax.broadcasted_iota(jnp.int32, (size, size), 1) // 64
    return jnp.where(row == col, 1.0 / 64.0, 0.0).astype(BF16)


def unit(p, mean_matrix):
    square = (p * p).astype(BF16)
    return (p * lax.rsqrt(dot(square, mean_matrix) + UNIT_EPS)).astype(BF16)


def pair_scores(q, k):
    low = lax.broadcasted_iota(jnp.int32, q.shape, 1) < 64
    zero = jnp.zeros_like(q)
    return dot_t(jnp.concatenate([jnp.where(low, q, zero), jnp.where(low, zero, q)], axis=0), k)


def pair_terms(scores, mask, scale_even, scale_odd):
    rows = scores.shape[0] // 2
    even = jnp.exp2(scores[:rows] * scale_even) * mask
    odd = jnp.exp2(scores[rows:] * scale_odd) * mask
    return jnp.concatenate([even, odd], axis=0).astype(BF16)


def pair_result(terms, v):
    rows = v.shape[0]
    low = lax.broadcasted_iota(jnp.int32, v.shape, 1) < 64
    sums = dot(terms, jnp.concatenate([v, jnp.ones_like(v)], axis=1))
    number = jnp.where(low, sums[:rows, :128], sums[rows:, :128])
    denom = jnp.where(low, sums[:rows, 128:], sums[rows:, 128:])
    return (number / denom).astype(BF16)


def pair_attend(q, k, v, mask, scale_even, scale_odd):
    return pair_result(pair_terms(pair_scores(q, k), mask, scale_even, scale_odd), v)


def shift_cols(t, step, axis):
    return pltpu.roll(t, step % t.shape[axis], axis)


def conv_kernel(block, top_ref, bot_ref, up_ref, down_ref, k_ref, part_ref, mate_ref, far_ref):
    lat = lax.axis_index("lat")
    last = lax.axis_size("lat") - 1
    has_up = (lat > 0).astype(F32)
    has_down = (lat < last).astype(F32)
    even = lax.axis_index("comp") == 0
    first_col = lax.broadcasted_iota(jnp.int32, (COLS, WIDTH), 0) == 0
    final_col = lax.broadcasted_iota(jnp.int32, (COLS, WIDTH), 0) == COLS - 1

    def tap(i, j):
        return k_ref[i, j, block : block + 1, :]

    for m in range(2):
        rows = [
            up_ref[m].astype(F32) * has_up,
            top_ref[m].astype(F32),
            bot_ref[m].astype(F32),
            down_ref[m].astype(F32) * has_down,
        ]
        for r in range(2):
            a, b, c = rows[r : r + 3]
            mid = tap(0, 1) * a + (tap(1, 1) + 1.0) * b + tap(2, 1) * c
            west = tap(0, 0) * a + tap(1, 0) * b + tap(2, 0) * c
            east = tap(0, 2) * a + tap(1, 2) * b + tap(2, 2) * c
            right = west[COLS - 1 :, :]
            left = east[:1, :]
            i = 2 * m + r
            mate_ref[i : i + 1, :] = jnp.where(even, right, left)
            far_ref[i : i + 1, :] = jnp.where(even, left, right)
            part_ref[m, r] = (
                mid
                + jnp.where(first_col, 0.0, shift_cols(west, 1, 0))
                + jnp.where(final_col, 0.0, shift_cols(east, -1, 0))
            )


def conv_call(block, top, bot, up, down, kernels):
    shape = (2, 2, COLS, WIDTH)
    return pl.pallas_call(
        lambda *refs: conv_kernel(block, *refs),
        out_shape=(
            pltpu.VMEM(shape, F32),
            pltpu.VMEM((4, WIDTH), F32),
            pltpu.VMEM((4, WIDTH), F32),
        ),
        in_specs=[VM] * 5,
        out_specs=(VM,) * 3,
        compiler_params=PARAMS,
    )(*near(top, bot, up, down, kernels))


def block_body(block, scale_ref, part_ref, mate_ref, far_ref, mask_ref, gain_ref, mlp_gain_ref,
               min_ref, mout_ref, weights, store):
    qkv_ref, out_ref, up_ref, down_ref = weights
    first_col = lax.broadcasted_iota(jnp.int32, (COLS, WIDTH), 0) == 0
    final_col = lax.broadcasted_iota(jnp.int32, (COLS, WIDTH), 0) == COLS - 1
    mean_matrix = head_mean(256)
    even = lax.axis_index("comp") == 0
    rows = []
    for m in range(2):
        for r in range(2):
            i = 2 * m + r
            x = part_ref[m, r]
            mate = mate_ref[i : i + 1, :]
            far = far_ref[i : i + 1, :]
            x = x + jnp.where(first_col, jnp.where(even, far, mate), 0.0)
            x = x + jnp.where(final_col, jnp.where(even, mate, far), 0.0)
            rows.append(x.astype(BF16))
    mixed = jnp.concatenate(rows, axis=0).astype(F32)
    normed = norm_rows(mixed, gain_ref[block : block + 1, :]).astype(BF16)
    qkv = dot(normed, qkv_ref())
    units = [unit(qkv[:, 256 * i : 256 * i + 256], mean_matrix) for i in range(3)]
    value = qkv[:, 2 * WIDTH :].astype(BF16)

    def lanes(j):
        return units[j // 2][:, 128 * (j % 2) : 128 * (j % 2) + 128]

    scales = [
        scale_ref[block : block + 1, h : h + 1] * (LOG2E / 64) for h in range(HEADS)
    ]
    row_out = []
    for first in range(0, 4, GROUP):
        cells = [(i, j) for i in range(first, first + GROUP) for j in range(3)]
        spans = {i: slice(COLS * i, COLS * i + COLS) for i in range(first, first + GROUP)}
        scores = [pair_scores(lanes(j)[spans[i]], lanes(3 + j)[spans[i]]) for i, j in cells]
        terms = [
            pair_terms(x, mask_ref[i % 2], scales[2 * j], scales[2 * j + 1])
            for x, (i, j) in zip(scores, cells)
        ]
        results = [
            pair_result(t, value[spans[i], 128 * j : 128 * j + 128])
            for t, (i, j) in zip(terms, cells)
        ]
        for i in range(GROUP):
            row_out.append(jnp.concatenate(results[3 * i : 3 * i + 3], axis=1))
    attended = jnp.concatenate(row_out, axis=0)
    after = (mixed + dot(attended, out_ref())).astype(BF16)
    after_f = after.astype(F32)
    scaled = norm_rows(after_f, mlp_gain_ref[block : block + 1, :])
    scaled = jnp.concatenate(
        [
            (scaled[: 2 * COLS] * min_ref[block, 0:1, :]).astype(BF16),
            (scaled[2 * COLS :] * min_ref[block, 1:2, :]).astype(BF16),
        ],
        axis=0,
    )
    total = after_f
    for h in range(0, HIDDEN, STEP):
        lifted = dot(scaled, up_ref(h, STEP))
        active = jnp.concatenate(
            [
                gelu(lifted[: 2 * COLS] * mout_ref[block, 0:1, h : h + STEP]).astype(BF16),
                gelu(lifted[2 * COLS :] * mout_ref[block, 1:2, h : h + STEP]).astype(BF16),
            ],
            axis=0,
        )
        total = total + dot(active, down_ref(h, STEP))
    store(total.astype(BF16))


def weight_getters(refs):
    return (
        lambda: refs[0][...],
        lambda: refs[1][...],
        lambda h, n: refs[2][:, h : h + n],
        lambda h, n: refs[3][h : h + n, :],
    )


def first_kernel(scale_ref, part_ref, mate_ref, far_ref, mask_ref, gain_ref, mlp_gain_ref, min_ref,
                 mout_ref, qkv_h, out_h, up_h, down_h, top_ref, bot_ref):
    weights = weight_getters((qkv_h, out_h, up_h, down_h))

    def store(value):
        for m in range(2):
            top_ref[m] = value[2 * m * COLS : (2 * m + 1) * COLS]
            bot_ref[m] = value[(2 * m + 1) * COLS : (2 * m + 2) * COLS]

    block_body(0, scale_ref, part_ref, mate_ref, far_ref, mask_ref, gain_ref, mlp_gain_ref,
               min_ref, mout_ref, weights, store)


def turned(value, straight):
    back = jnp.concatenate([value[j : j + 1] for j in reversed(range(value.shape[0]))], axis=0)
    return jnp.where(straight, value, back)


def second_kernel(scale_ref, part_ref, mate_ref, far_ref, mask_ref, gain_ref, mlp_gain_ref, min_ref,
                  mout_ref, qkv_h, out_h, up_h, down_h, prev_ref, sea_ref, flux_ref,
                  cur_ref, start_ref):
    weights = weight_getters((qkv_h, out_h, up_h, down_h))

    straight = lax.axis_index("comp") == 0

    def store(value):
        flux = dot(value, flux_ref[...])
        for i in range(4):
            m, r = i // 2, i % 2
            at = slice(COLS * i, COLS * i + COLS)
            cur_ref[m, r] = value[at]
            start = sea_ref[r] * (prev_ref[m, r].astype(F32) + flux[at])
            start_ref[:, i] = turned(start.reshape(16, 8, OCEAN), straight).astype(BF16)

    block_body(1, scale_ref, part_ref, mate_ref, far_ref, mask_ref, gain_ref, mlp_gain_ref,
               min_ref, mout_ref, weights, store)


def first_call(*args):
    row = pltpu.VMEM((2, COLS, WIDTH), BF16)
    return pl.pallas_call(
        first_kernel,
        out_shape=(row, row),
        in_specs=[VM] * 13,
        out_specs=(VM, VM),
        compiler_params=PARAMS,
        name="block_0",
    )(*near(*args))


def second_call(*args):
    return pl.pallas_call(
        second_kernel,
        out_shape=(
            pltpu.VMEM((2, 2, COLS, WIDTH), BF16),
            pltpu.VMEM((16, 4, 8, OCEAN), BF16),
        ),
        in_specs=[VM] * 16,
        out_specs=(VM, VM),
        compiler_params=PARAMS,
        name="block_1",
    )(*near(*args))


def taps3(field, k_ref, index):
    zero = jnp.zeros_like(field[:1])
    above = jnp.concatenate([zero, field[:-1]], axis=0)
    below = jnp.concatenate([field[1:], zero], axis=0)

    def column(j):
        return (
            k_ref[index, 0, j : j + 1, :] * above
            + k_ref[index, 1, j : j + 1, :] * field
            + k_ref[index, 2, j : j + 1, :] * below
        )

    return column(1) + shift_cols(column(0), 1, 1) + shift_cols(column(2), -1, 1)


def ocean_kernel(scale_ref, own_ref, pair_ref, next_ref, k_ref, point_ref, gain_ref, qkv_ref,
                 out_ref, last_ref, pool_ref, wide_ref):
    mean_matrix = head_mean(128)
    row = lax.broadcasted_iota(jnp.int32, (128, 128), 0) % 8
    col = lax.broadcasted_iota(jnp.int32, (128, 128), 1) % 8
    mask = jnp.where(row == col, 1.0, 0.0)
    wide_ref[...] = jnp.zeros_like(wide_ref)
    first_of_pair = (lax.axis_index("lat") + lax.axis_index("comp")) % 2 == 0
    for m in range(2):
        def rows_of(ref):
            even = ref[:, 2 * m].astype(F32)[:, None]
            odd = ref[:, 2 * m + 1].astype(F32)[:, None]
            return jnp.concatenate([even, odd], axis=1).reshape(32, 8, OCEAN)

        pair = rows_of(pair_ref)
        following = rows_of(next_ref)
        west = jnp.where(first_of_pair, following, pair)
        east = jnp.where(first_of_pair, pair, following)
        field = jnp.concatenate([west, rows_of(own_ref), east], axis=1)
        act = taps3(field, k_ref, 0).astype(BF16).reshape(32 * 24, OCEAN)
        fine = gelu(dot(act, point_ref[0])).astype(BF16).astype(F32)
        fine4 = fine.reshape(16, 2, 24, OCEAN)
        pool_ref[...] = (fine4[:, 0] + fine4[:, 1]).reshape(16 * 24, OCEAN)
        coarse = []
        for i in range(16):
            coarse.append(
                pool_ref[pl.ds(24 * i + 4, 8, stride=2), :]
                + pool_ref[pl.ds(24 * i + 5, 8, stride=2), :]
            )
        coarse = (jnp.concatenate(coarse, axis=0) * 0.25).astype(BF16).astype(F32)
        act = taps3(coarse.reshape(16, 8, OCEAN), k_ref, 1).astype(BF16).reshape(128, OCEAN)
        first = gelu(dot(act, point_ref[1])).astype(BF16).astype(F32)
        normed = norm_rows(first, gain_ref[...]).astype(BF16)
        qkv = dot(normed, qkv_ref[...])
        attended = pair_attend(
            unit(qkv[:, :128], mean_matrix),
            unit(qkv[:, 128:256], mean_matrix),
            qkv[:, 256:].astype(BF16),
            mask,
            scale_ref[:, 0:1] * (LOG2E / 64),
            scale_ref[:, 1:2] * (LOG2E / 64),
        )
        following = (first + dot(attended, out_ref[...])).astype(BF16).astype(F32)
        for i in range(16):
            piece = following[8 * i : 8 * i + 8]
            wide_ref[pl.ds(24 * i + 4, 8, stride=2), :] = piece
            wide_ref[pl.ds(24 * i + 5, 8, stride=2), :] = piece
        spread = wide_ref[...].reshape(16, 1, 24, OCEAN)
        merged = (fine4 + spread).astype(BF16).astype(F32).reshape(32, 24, OCEAN)
        act = taps3(merged, k_ref, 2)[:, 8:16].astype(BF16).reshape(16, 2, 8, OCEAN)
        last_ref[:, 2 * m] = act[:, 0]
        last_ref[:, 2 * m + 1] = act[:, 1]


def ocean_call(*args):
    return pl.pallas_call(
        ocean_kernel,
        out_shape=pltpu.VMEM((16, 4, 8, OCEAN), BF16),
        in_specs=[VM] * 9,
        out_specs=VM,
        compiler_params=PARAMS,
        scratch_shapes=[pltpu.VMEM((16 * 24, OCEAN), F32), pltpu.VMEM((16 * 24, OCEAN), F32)],
        name="ocean",
    )(*near(*args))


def final_kernel(last_ref, start_ref, cur_ref, sea_ref, point_ref, return_ref, air_hbm, water_hbm,
                 air_ref, water_ref, sems):
    copies = []
    straight = lax.axis_index("comp") == 0
    for m in range(2):
        for r in range(2):
            i = 2 * m + r
            act = turned(last_ref[:, i].astype(F32), straight).astype(BF16).reshape(COLS, OCEAN)
            start = turned(start_ref[:, i].astype(F32), straight).reshape(COLS, OCEAN)
            lifted = gelu(dot(act, point_ref[2]))
            sea = sea_ref[r]
            water = (sea * (start + lifted)).astype(BF16)
            water_ref[m, r] = water
            back = dot(water, return_ref[...])
            sea3 = jnp.concatenate([sea, sea, sea], axis=1)
            air_ref[m, r] = (cur_ref[m, r].astype(F32) + sea3 * back).astype(BF16)
            for k, (src, dst) in enumerate(((water_ref, water_hbm), (air_ref, air_hbm))):
                copies.append(pltpu.make_async_copy(src.at[m, r], dst.at[m, r], sems.at[2 * i + k]))
                copies[-1].start()
    for copy in copies:
        copy.wait()


def final_call(*args):
    return pl.pallas_call(
        final_kernel,
        out_shape=(
            jax.ShapeDtypeStruct((2, 2, COLS, WIDTH), BF16),
            jax.ShapeDtypeStruct((2, 2, COLS, OCEAN), BF16),
        ),
        in_specs=[VM] * 6,
        out_specs=(ANY, ANY),
        scratch_shapes=[
            pltpu.VMEM((2, 2, COLS, WIDTH), BF16),
            pltpu.VMEM((2, 2, COLS, OCEAN), BF16),
            pltpu.SemaphoreType.DMA((8,)),
        ],
        compiler_params=PARAMS,
        name="final",
    )(*near(*args))


LON = ("lon", "comp")


def ring(count, step):
    return [(i, (i + step) % count) for i in range(count)]


def group_swap(first):
    lats = lax.axis_size("lat")
    sectors = lax.axis_size("lon") * lax.axis_size("comp")
    total = lats * sectors

    def device(g):
        sector, place = g // lats, g % lats
        lat = place if sector % 2 == 0 else lats - 1 - place
        return lat * sectors + sector

    pairs = []
    for g in range(first, total, 2):
        a, b = device(g), device((g + 1) % total)
        pairs += [(a, b), (b, a)]
    return sorted(pairs)


def mix(block, top, bot, kernels):
    lats = lax.axis_size("lat")
    sectors = lax.axis_size("lon") * lax.axis_size("comp")
    up = lax.ppermute(bot, "lat", ring(lats, 1))
    down = lax.ppermute(top, "lat", ring(lats, -1))
    part, mate, far = conv_call(block, top, bot, up, down, kernels)
    far = lax.ppermute(far, LON, [(i, (i + 2 * (i % 2) - 1) % sectors) for i in range(sectors)])
    mate = lax.ppermute(mate, LON, [(i, i ^ 1) for i in range(sectors)])
    return part, mate, far


def start_copies(sources, targets, sems):
    copies = [
        pltpu.make_async_copy(src, dst, sems.at[i]) for i, (src, dst) in enumerate(zip(sources, targets))
    ]
    for copy in copies:
        copy.start()
    return copies


def load_kernel(block, count, *refs):
    sources = [
        ref if i < count - 4 else ref.at[block] for i, ref in enumerate(refs[:count])
    ]
    if block == 0:
        mask_ref, sea_ref = refs[count : count + 2]
        ids_ref, land_ref, sems = refs[-3:]
        targets = (ids_ref, land_ref) + tuple(refs[count + 2 : -3])
        copies = start_copies(sources, targets, sems)
        for copy in copies[:2]:
            copy.wait()
        for r in range(2):
            ids = jnp.broadcast_to(ids_ref[r : r + 1, :].astype(F32), (COLS, COLS))
            mask_ref[r] = (ids == ids.T).astype(F32)
            sea_ref[r] = jnp.broadcast_to(land_ref[r : r + 1, :].astype(F32), (COLS, COLS)).T
        copies = copies[2:]
    else:
        copies = start_copies(sources, refs[count:-1], refs[-1])
    for copy in copies:
        copy.wait()


def load_call(block, *arrays):
    count = len(arrays)
    shapes = [a.shape for a in arrays[:-4]] + [a.shape[1:] for a in arrays[-4:]]
    outs = [pltpu.VMEM(s, a.dtype) for s, a in zip(shapes, arrays)]
    scratch = [pltpu.SemaphoreType.DMA((count,))]
    if block == 0:
        outs = [pltpu.VMEM((2, COLS, COLS), F32)] * 2 + outs[2:]
        scratch = [pltpu.VMEM((2, COLS), jnp.int32), pltpu.VMEM((2, COLS), jnp.int32)] + scratch
    return pl.pallas_call(
        lambda *refs: load_kernel(block, count, *refs),
        out_shape=outs,
        in_specs=[ANY] * count,
        out_specs=[VM] * len(outs),
        scratch_shapes=scratch,
        compiler_params=PARAMS,
    )(*(pltpu.with_memory_space_constraint(a, pltpu.HBM) for a in arrays))


def per_device(atm_state, ocean_prev, land_sea, window_ids, conv_atm, attn_gain, qkv_matrix,
               attn_scales, out_matrix, mlp_gain, member_in, member_out, up_matrix, down_matrix,
               flux_matrix, conv_ocean, point_matrix, ocean_gain, ocean_qkv, ocean_scale, ocean_out,
               seaside_return_matrix):
    big = (qkv_matrix, out_matrix, up_matrix, down_matrix)
    mask, sea, conv_atm, attn_scales, attn_gain, mlp_gain, member_in, member_out, *weights = load_call(
        0, window_ids, land_sea, jnp.transpose(conv_atm, (1, 2, 0, 3)), attn_scales, attn_gain,
        mlp_gain, member_in, member_out, *big
    )
    small = (attn_gain, mlp_gain, member_in, member_out)
    part, mate, far = mix(0, atm_state[:, 0], atm_state[:, 1], conv_atm)
    top, bot = first_call(attn_scales, part, mate, far, mask, *small, *weights)

    (ocean_prev, flux_matrix, conv_ocean, point_matrix, ocean_gain, ocean_qkv, ocean_scale, ocean_out,
     seaside_return_matrix, *weights) = load_call(
        1, ocean_prev, flux_matrix, conv_ocean, point_matrix, ocean_gain[None, :], ocean_qkv,
        ocean_scale[None, :], ocean_out, seaside_return_matrix, *big
    )
    part, mate, far = mix(1, top, bot, conv_atm)
    current, start = second_call(
        attn_scales, part, mate, far, mask, *small, *weights, ocean_prev, sea, flux_matrix
    )
    own = lax.all_to_all(start, "lat", 0, 0)
    axes = ("lat",) + LON
    pair = lax.ppermute(own, axes, group_swap(0))
    following = lax.ppermute(own, axes, group_swap(1))
    last = ocean_call(ocean_scale, own, pair, following, conv_ocean, point_matrix,
                      ocean_gain, ocean_qkv, ocean_out)
    last = lax.all_to_all(last, "lat", 0, 0)
    return final_call(last, start, current, sea, point_matrix, seaside_return_matrix)


def solution(mesh):
    field = P(None, "lat", LON, None)
    column = P("lat", LON)
    return jax.shard_map(
        per_device,
        mesh=mesh,
        in_specs=(field, field, column, column) + (P(),) * 18,
        out_specs=(field, field),
        check_vma=False,
    )
```

profile of v0, /device:TPU:32, one launch (start us, length us, event | category | flops | bytes accessed | tf_op | source)
XLA Modules:
  0.0 85.4 jit_solution(13133451707496242835)
XLA Ops:
  0.6 1.1 %slice_bitcast_fusion = (bf16[2,128,384]{2,1,0:T(8,128)(2,1)S(1)}, bf16[2,128,384]{2,1,0:T(8,128)(2,1)S(1)}) fusion(bf16[2,2,128,384]{3,2,1,0:T(8,128)(2,1)} %param.22), kind=kLoop, calls=%fused_computation | loop fusion | bytes 786432 | tf_op jit(solution)/shard_map/squeeze | solution.py:501
  1.7 2.0 %collective-permute-start = (bf16[2,128,384]{2,1,0:T(8,128)(2,1)S(1)}, bf16[2,128,384]{2,1,0:T(8,128)(2,1)S(1)}, u32[]{:S(2)}, u32[]{:S(2)}) collective-permute-start(bf16[2,128,384]{2,1,0:T(8,128)(2,1)S(1)} %get-tuple-element.72.refs_1_), channel_id=1, source_target_pairs={{0,16},{16,32},{32,48},{48,64},{64,80},{80,96},{96,112},{112,128},... | collective-permute-start | bytes 589832 | tf_op jit(solution)/shard_map/ppermute | solution.py:434
  3.7 0.1 collective-permute-start.1
  3.8 2.2 %shard_map.222 = (f32[2,128,128]{2,1,0:T(8,128)S(1)}, f32[2,128,128]{2,1,0:T(8,128)S(1)}, f32[3,3,2,384]{3,2,1,0:T(2,128)S(1)}, f32[2,6]{1,0:T(2,128)S(1)}, f32[...) custom-call(s32[2,128]{1,0:T(2,128)} %refs_0_.3, ...), custom_call_target="tpu_custom_call" | custom-call | tf_op jit(solution)/shard_map/pallas_call | solution.py:481
  6.0 2.4 %collective-permute-done.refs_2_ = bf16[2,128,384]{2,1,0:T(8,128)(2,1)S(1)} collective-permute-done((bf16[2,128,384]{2,1,0:T(8,128)(2,1)S(1)}, bf16[2,128,384]{2,1,0:T(8,128)(2,1)S(1)}, u32[]{:S(2)}, u32[]{:S(2)}) %collective-permute-start) | collective-permute-done | bytes 196640 | tf_op jit(solution)/shard_map/ppermute | solution.py:434
  8.4 1.8 %collective-permute-done.1.refs_3_ = bf16[2,128,384]{2,1,0:T(8,128)(2,1)S(1)} collective-permute-done((bf16[2,128,384]{2,1,0:T(8,128)(2,1)S(1)}, bf16[2,128,384]{2,1,0:T(8,128)(2,1)S(1)}, u32[]{:S(2)}, u32[]{:S(2)}) %collective-permute-start.1) | collective-permute-done | bytes 196640 | tf_op jit(solution)/shard_map/ppermute | solution.py:435
  10.2 0.7 shard_map.223
  10.9 0.1 collective-permute-start.2
  11.0 5.5 %collective-permute-start.3 = (f32[4,384]{1,0:T(4,128)S(1)}, f32[4,384]{1,0:T(4,128)S(1)}, u32[]{:S(2)}, u32[]{:S(2)}) collective-permute-start(f32[4,384]{1,0:T(4,128)S(1)} %get-tuple-element.42), channel_id=1, source_target_pairs={{0,15},{1,2},{2,1},{3,4},{4,3},{5,6},{6,5},{7,8},{8,7},{9,10},{10,... | collective-permute-start | bytes 18440 | tf_op jit(solution)/shard_map/ppermute | solution.py:437
  16.5 0.0 collective-permute-done.2.mate_ref
  16.5 1.3 %collective-permute-done.3.far_ref = f32[4,384]{1,0:T(4,128)S(1)} collective-permute-done((f32[4,384]{1,0:T(4,128)S(1)}, f32[4,384]{1,0:T(4,128)S(1)}, u32[]{:S(2)}, u32[]{:S(2)}) %collective-permute-start.3) | collective-permute-done | bytes 6176 | tf_op jit(solution)/shard_map/ppermute | solution.py:437
  17.9 4.3 %block_0.1 = (bf16[2,128,384]{2,1,0:T(8,128)(2,1)S(1)}, bf16[2,128,384]{2,1,0:T(8,128)(2,1)S(1)}) custom-call(f32[2,6]{1,0:T(2,128)S(1)} %get-tuple-element.38.scale_ref, f32[2,2,128,384]{3,2,1,0:T(8,128)S(1)} %get-tuple-element.40.part_ref, f32[4,384]{1,0:T(4,128)S(1)} %collective-permute-done.2.mate_ref, f32[4,384]{1,0:T(4,128)S(1)} %collective-permute-done.3.far_ref, ...), custom_call_target="tpu_custom_call" | custom-call | tf_op jit(solution)/shard_map/block_0/pallas_call | solution.py:260
  22.2 3.4 %collective-permute-start.5 = (bf16[2,128,384]{2,1,0:T(8,128)(2,1)S(1)}, bf16[2,128,384]{2,1,0:T(8,128)(2,1)S(1)}, u32[]{:S(2)}, u32[]{:S(2)}) collective-permute-start(bf16[2,128,384]{2,1,0:T(8,128)(2,1)S(1)} %get-tuple-element.52.refs_0_), channel_id=1, source_target_pairs={{0,240},{16,0},{32,16},{48,32},{64,48},{80,64},{96,80},{112,96},{1... | collective-permute-start | bytes 589832 | tf_op jit(solution)/shard_map/ppermute | solution.py:435
  25.6 0.0 collective-permute-start.4
  25.6 3.4 %collective-permute-done.5.refs_3_ = bf16[2,128,384]{2,1,0:T(8,128)(2,1)S(1)} collective-permute-done((bf16[2,128,384]{2,1,0:T(8,128)(2,1)S(1)}, bf16[2,128,384]{2,1,0:T(8,128)(2,1)S(1)}, u32[]{:S(2)}, u32[]{:S(2)}) %collective-permute-start.5) | collective-permute-done | bytes 196640 | tf_op jit(solution)/shard_map/ppermute | solution.py:435
  29.1 4.1 %collective-permute-done.4.refs_2_ = bf16[2,128,384]{2,1,0:T(8,128)(2,1)S(1)} collective-permute-done((bf16[2,128,384]{2,1,0:T(8,128)(2,1)S(1)}, bf16[2,128,384]{2,1,0:T(8,128)(2,1)S(1)}, u32[]{:S(2)}, u32[]{:S(2)}) %collective-permute-start.4) | collective-permute-done | bytes 196640 | tf_op jit(solution)/shard_map/ppermute | solution.py:434
  33.2 0.7 shard_map.224
  33.9 0.1 collective-permute-start.6
  34.0 4.8 %collective-permute-start.7 = (f32[4,384]{1,0:T(4,128)S(1)}, f32[4,384]{1,0:T(4,128)S(1)}, u32[]{:S(2)}, u32[]{:S(2)}) collective-permute-start(f32[4,384]{1,0:T(4,128)S(1)} %get-tuple-element.56), channel_id=1, source_target_pairs={{0,15},{1,2},{2,1},{3,4},{4,3},{5,6},{6,5},{7,8},{8,7},{9,10},{10,... | collective-permute-start | bytes 18440 | tf_op jit(solution)/shard_map/ppermute | solution.py:437
  38.8 2.4 %shard_map.221 = (bf16[2,2,128,128]{3,2,1,0:T(8,128)(2,1)S(1)}, bf16[384,128]{1,0:T(8,128)(2,1)S(1)}, f32[3,3,3,128]{3,2,1,0:T(4,128)S(1)}, bf16[3,128,128]{2,1,...) custom-call(bf16[2,2,128,128]{3,2,1,0:T(8,128)(2,1)} %refs_0_.2, ...), custom_call_target="tpu_custom_call" | custom-call | tf_op jit(solution)/shard_map/pallas_call | solution.py:481
  41.2 0.0 collective-permute-done.6.mate_ref
  41.2 0.0 collective-permute-done.7.far_ref
  41.2 4.5 %block_1.1 = (bf16[2,2,128,384]{3,2,1,0:T(8,128)(2,1)S(1)}, bf16[16,4,8,128]{3,2,1,0:T(8,128)(2,1)S(1)}) custom-call(f32[2,6]{1,0:T(2,128)S(1)} %get-tuple-element.38.scale_ref, f32[2,2,128,384]{3,2,1,0:T(8,128)S(1)} %get-tuple-element.54.part_ref, f32[4,384]{1,0:T(4,128)S(1)} %collective-permute-done.6.mate_ref, ...), custom_call_target="tpu_custom_call" | custom-call | tf_op jit(solution)/shard_map/block_1/pallas_call | solution.py:271
  45.7 15.3 %all_to_all.10.own_ref = bf16[16,4,8,128]{3,2,1,0:T(8,128)(2,1)S(1)} all-to-all(bf16[16,4,8,128]{3,2,1,0:T(8,128)(2,1)S(1)} %get-tuple-element.64.start_ref), channel_id=1, replica_groups=mesh['lat'=16,'lon'=8,'comp'=2] {'lat'}, dimensions={0} | all-to-all | bytes 262144 | tf_op jit(solution)/shard_map/all_to_all | solution.py:513
  61.0 0.7 collective-permute-start.9
  61.8 3.2 %collective-permute-start.8 = (bf16[16,4,8,128]{3,2,1,0:T(8,128)(2,1)S(1)}, bf16[16,4,8,128]{3,2,1,0:T(8,128)(2,1)S(1)}, u32[]{:S(2)}, u32[]{:S(2)}) collective-permute-start(bf16[16,4,8,128]{3,2,1,0:T(8,128)(2,1)S(1)} %all_to_all.10.own_ref), channel_id=1, source_target_pairs={{0,16},{1,17},{2,18},{3,19},{4,20},{5,21},{6,22},{7,23},{8,24},{9,... | collective-permute-start | bytes 393224 | tf_op jit(solution)/shard_map/ppermute | solution.py:515
  64.9 1.1 %collective-permute-done.9.next_ref = bf16[16,4,8,128]{3,2,1,0:T(8,128)(2,1)S(1)} collective-permute-done((bf16[16,4,8,128]{3,2,1,0:T(8,128)(2,1)S(1)}, bf16[16,4,8,128]{3,2,1,0:T(8,128)(2,1)S(1)}, u32[]{:S(2)}, u32[]{:S(2)}) %collective-permute-start.9) | collective-permute-done | bytes 131104 | tf_op jit(solution)/shard_map/ppermute | solution.py:516
  66.0 1.9 %collective-permute-done.8.pair_ref = bf16[16,4,8,128]{3,2,1,0:T(8,128)(2,1)S(1)} collective-permute-done((bf16[16,4,8,128]{3,2,1,0:T(8,128)(2,1)S(1)}, bf16[16,4,8,128]{3,2,1,0:T(8,128)(2,1)S(1)}, u32[]{:S(2)}, u32[]{:S(2)}) %collective-permute-start.8) | collective-permute-done | bytes 131104 | tf_op jit(solution)/shard_map/ppermute | solution.py:515
  67.9 3.0 %ocean.1 = bf16[16,4,8,128]{3,2,1,0:T(8,128)(2,1)S(1)} custom-call(f32[1,2]{1,0:T(1,128)S(1)} %get-tuple-element.37.scale_ref, bf16[16,4,8,128]{3,2,1,0:T(8,128)(2,1)S(1)} %all_to_all.10.own_ref, bf16[16,4,8,128]{3,2,1,0:T(8,128)(2,1)S(1)} %collective-permute-done.8.pair_ref, bf16[16,4,8,128]{3,2,1,0:T(8,128)(2,1)S(1)} %collective-permute-done.9.next_ref, ...), custom_call_target="tpu_custom_call" | custom-call | tf_op jit(solution)/shard_map/ocean/pallas_call | solution.py:354
  70.9 12.8 %all_to_all.11.last_ref = bf16[16,4,8,128]{3,2,1,0:T(8,128)(2,1)S(1)} all-to-all(bf16[16,4,8,128]{3,2,1,0:T(8,128)(2,1)S(1)} %ocean.1), channel_id=1, replica_groups=mesh['lat'=16,'lon'=8,'comp'=2] {'lat'}, dimensions={0} | all-to-all | bytes 262144 | tf_op jit(solution)/shard_map/all_to_all | solution.py:519
  83.7 1.5 %final.1 = (bf16[2,2,128,384]{3,2,1,0:T(8,128)(2,1)}, bf16[2,2,128,128]{3,2,1,0:T(8,128)(2,1)}) custom-call(bf16[16,4,8,128]{3,2,1,0:T(8,128)(2,1)S(1)} %all_to_all.11.last_ref, bf16[16,4,8,128]{3,2,1,0:T(8,128)(2,1)S(1)} %get-tuple-element.64.start_ref, bf16[2,2,128,384]{3,2,1,0:T(8,128)(2,1)S(1)} %get-tuple-element.70.cur_ref, ...), custom_call_target="tpu_custom_call" | custom-call | tf_op jit(solution)/shard_map/final/pallas_call | solution.py:389
Async XLA Ops:
  1.7 6.7 %collective-permute-start = (bf16[2,128,384]{2,1,0:T(8,128)(2,1)S(1)}, bf16[2,128,384]{2,1,0:T(8,128)(2,1)S(1)}, u32[]{:S(2)}, u32[]{:S(2)}) collective-permute-start(bf16[2,128,384]{2,1,0:T(8,128)(2,1)S(1)} %get-tuple-element.72.refs_1_), channel_id=1, source_target_pairs={{0,16},{16,32},{32,48},{48,64},{64,80},{80,96},{96,112},{112,128},... | collective-permute-start | bytes 589832 | tf_op jit(solution)/shard_map/ppermute | solution.py:434
  3.7 6.5 %collective-permute-start.1 = (bf16[2,128,384]{2,1,0:T(8,128)(2,1)S(1)}, bf16[2,128,384]{2,1,0:T(8,128)(2,1)S(1)}, u32[]{:S(2)}, u32[]{:S(2)}) collective-permute-start(bf16[2,128,384]{2,1,0:T(8,128)(2,1)S(1)} %get-tuple-element.73.refs_0_), channel_id=1, source_target_pairs={{0,240},{16,0},{32,16},{48,32},{64,48},{80,64},{96,80},{112,96},{1... | collective-permute-start | bytes 589832 | tf_op jit(solution)/shard_map/ppermute | solution.py:435
  10.9 5.6 %collective-permute-start.2 = (f32[4,384]{1,0:T(4,128)S(1)}, f32[4,384]{1,0:T(4,128)S(1)}, u32[]{:S(2)}, u32[]{:S(2)}) collective-permute-start(f32[4,384]{1,0:T(4,128)S(1)} %get-tuple-element.41), channel_id=1, source_target_pairs={{0,1},{1,0},{2,3},{3,2},{4,5},{5,4},{6,7},{7,6},{8,9},{9,8},{10,11... | collective-permute-start | bytes 18440 | tf_op jit(solution)/shard_map/ppermute | solution.py:438
  11.0 6.8 %collective-permute-start.3 = (f32[4,384]{1,0:T(4,128)S(1)}, f32[4,384]{1,0:T(4,128)S(1)}, u32[]{:S(2)}, u32[]{:S(2)}) collective-permute-start(f32[4,384]{1,0:T(4,128)S(1)} %get-tuple-element.42), channel_id=1, source_target_pairs={{0,15},{1,2},{2,1},{3,4},{4,3},{5,6},{6,5},{7,8},{8,7},{9,10},{10,... | collective-permute-start | bytes 18440 | tf_op jit(solution)/shard_map/ppermute | solution.py:437
  22.2 6.9 %collective-permute-start.5 = (bf16[2,128,384]{2,1,0:T(8,128)(2,1)S(1)}, bf16[2,128,384]{2,1,0:T(8,128)(2,1)S(1)}, u32[]{:S(2)}, u32[]{:S(2)}) collective-permute-start(bf16[2,128,384]{2,1,0:T(8,128)(2,1)S(1)} %get-tuple-element.52.refs_0_), channel_id=1, source_target_pairs={{0,240},{16,0},{32,16},{48,32},{64,48},{80,64},{96,80},{112,96},{1... | collective-permute-start | bytes 589832 | tf_op jit(solution)/shard_map/ppermute | solution.py:435
  25.6 7.6 %collective-permute-start.4 = (bf16[2,128,384]{2,1,0:T(8,128)(2,1)S(1)}, bf16[2,128,384]{2,1,0:T(8,128)(2,1)S(1)}, u32[]{:S(2)}, u32[]{:S(2)}) collective-permute-start(bf16[2,128,384]{2,1,0:T(8,128)(2,1)S(1)} %get-tuple-element.53.refs_1_), channel_id=1, source_target_pairs={{0,16},{16,32},{32,48},{48,64},{64,80},{80,96},{96,112},{112,128},... | collective-permute-start | bytes 589832 | tf_op jit(solution)/shard_map/ppermute | solution.py:434
  33.9 7.3 %collective-permute-start.6 = (f32[4,384]{1,0:T(4,128)S(1)}, f32[4,384]{1,0:T(4,128)S(1)}, u32[]{:S(2)}, u32[]{:S(2)}) collective-permute-start(f32[4,384]{1,0:T(4,128)S(1)} %get-tuple-element.55), channel_id=1, source_target_pairs={{0,1},{1,0},{2,3},{3,2},{4,5},{5,4},{6,7},{7,6},{8,9},{9,8},{10,11... | collective-permute-start | bytes 18440 | tf_op jit(solution)/shard_map/ppermute | solution.py:438
  34.0 7.2 %collective-permute-start.7 = (f32[4,384]{1,0:T(4,128)S(1)}, f32[4,384]{1,0:T(4,128)S(1)}, u32[]{:S(2)}, u32[]{:S(2)}) collective-permute-start(f32[4,384]{1,0:T(4,128)S(1)} %get-tuple-element.56), channel_id=1, source_target_pairs={{0,15},{1,2},{2,1},{3,4},{4,3},{5,6},{6,5},{7,8},{8,7},{9,10},{10,... | collective-permute-start | bytes 18440 | tf_op jit(solution)/shard_map/ppermute | solution.py:437
  61.0 5.0 %collective-permute-start.9 = (bf16[16,4,8,128]{3,2,1,0:T(8,128)(2,1)S(1)}, bf16[16,4,8,128]{3,2,1,0:T(8,128)(2,1)S(1)}, u32[]{:S(2)}, u32[]{:S(2)}) collective-permute-start(bf16[16,4,8,128]{3,2,1,0:T(8,128)(2,1)S(1)} %all_to_all.10.own_ref), channel_id=1, source_target_pairs={{0,15},{1,2},{2,1},{3,4},{4,3},{5,6},{6,5},{7,8},{8,7},{9,10},{10,... | collective-permute-start | bytes 393224 | tf_op jit(solution)/shard_map/ppermute | solution.py:516
  61.8 6.1 %collective-permute-start.8 = (bf16[16,4,8,128]{3,2,1,0:T(8,128)(2,1)S(1)}, bf16[16,4,8,128]{3,2,1,0:T(8,128)(2,1)S(1)}, u32[]{:S(2)}, u32[]{:S(2)}) collective-permute-start(bf16[16,4,8,128]{3,2,1,0:T(8,128)(2,1)S(1)} %all_to_all.10.own_ref), channel_id=1, source_target_pairs={{0,16},{1,17},{2,18},{3,19},{4,20},{5,21},{6,22},{7,23},{8,24},{9,... | collective-permute-start | bytes 393224 | tf_op jit(solution)/shard_map/ppermute | solution.py:515
where the time goes:
time: 85.6 us; the launch traced here: 85.4 us
  blocking collectives  28.1 us (33%)
  starting transfers between devices  19.9 us (23%)
  Pallas kernels  19.3 us (23%)
  waiting for transfers between devices  16.1 us (19%)
  local copies, waits for them, and re-layouts  1.07 us (1%)
  between operations  0.88 us (1%)
    all_to_all x1, blocking collectives, per_device(): own = lax.all_to_all(start, 'lat', 0, 0)  15.3 us
    all_to_all x1, blocking collectives, per_device(): last = lax.all_to_all(last, 'lat', 0, 0)  12.8 us
    ppermute x2, starting transfers between devices, mix(): lax.ppermute(far, LON, [(i, (i + 2 * (i % 2) - 1) % sectors) for i in ran...  10.3 us
    ppermute x2, waiting for transfers between devices, mix(): up = lax.ppermute(bot, 'lat', ring(lats, 1))  6.54 us
    ppermute x2, waiting for transfers between devices, mix(): down = lax.ppermute(top, 'lat', ring(lats, -1))  5.24 us
    pallas_call x2, Pallas kernels, load_call(): pl.pallas_call(lambda *refs: load_kernel(block, count, *refs), out_shape=...  4.64 us
    pallas_call x1, Pallas kernels, second_call(): pl.pallas_call(second_kernel, out_shape=(pltpu.VMEM((2, 2, COLS, WIDTH),...  4.47 us
    pallas_call x1, Pallas kernels, first_call(): pl.pallas_call(first_kernel, out_shape=(row, row), in_specs=[VM] * 13, ou...  4.33 us
  transfers between devices with their start and end apart: 10, of which 7 were waited for; matrix products, arithmetic and copies ran while one was open for 0% of the time, Pallas kernels for 5%

commit v1 on v0

--- a/solution.py
+++ b/solution.py
@@ -88,12 +88,39 @@
     return pltpu.roll(t, step % t.shape[axis], axis)
 
 
-def conv_kernel(block, top_ref, bot_ref, up_ref, down_ref, k_ref, part_ref, mate_ref, far_ref):
+def edge_kernel(block, top_ref, bot_ref, up_ref, down_ref, k_ref, *refs):
+    mate_ref, far_ref = refs[-2:]
+    has_up, has_down = inner_rows()
+    even = lax.axis_index("comp") == 0
+
+    def tap(i, j):
+        return k_ref[i, j, block : block + 1, :]
+
+    for m in range(2):
+        def column(c):
+            return [
+                up_ref[m, c : c + 1, :].astype(F32) * has_up,
+                top_ref[m, c : c + 1, :].astype(F32),
+                bot_ref[m, c : c + 1, :].astype(F32),
+                down_ref[m, c : c + 1, :].astype(F32) * has_down,
+            ]
+
+        final, first = column(COLS - 1), column(0)
+        for r in range(2):
+            right = sum(tap(i, 0) * final[r + i] for i in range(3))
+            left = sum(tap(i, 2) * first[r + i] for i in range(3))
+            i = 2 * m + r
+            mate_ref[i : i + 1, :] = jnp.where(even, right, left)
+            far_ref[i : i + 1, :] = jnp.where(even, left, right)
+
+
+def inner_rows():
     lat = lax.axis_index("lat")
-    last = lax.axis_size("lat") - 1
-    has_up = (lat > 0).astype(F32)
-    has_down = (lat < last).astype(F32)
-    even = lax.axis_index("comp") == 0
+    return (lat > 0).astype(F32), (lat < lax.axis_size("lat") - 1).astype(F32)
+
+
+def conv_kernel(block, top_ref, bot_ref, up_ref, down_ref, k_ref, part_ref):
+    has_up, has_down = inner_rows()
     first_col = lax.broadcasted_iota(jnp.int32, (COLS, WIDTH), 0) == 0
     final_col = lax.broadcasted_iota(jnp.int32, (COLS, WIDTH), 0) == COLS - 1
 
@@ -112,11 +139,6 @@
             mid = tap(0, 1) * a + (tap(1, 1) + 1.0) * b + tap(2, 1) * c
             west = tap(0, 0) * a + tap(1, 0) * b + tap(2, 0) * c
             east = tap(0, 2) * a + tap(1, 2) * b + tap(2, 2) * c
-            right = west[COLS - 1 :, :]
-            left = east[:1, :]
-            i = 2 * m + r
-            mate_ref[i : i + 1, :] = jnp.where(even, right, left)
-            far_ref[i : i + 1, :] = jnp.where(even, left, right)
             part_ref[m, r] = (
                 mid
                 + jnp.where(first_col, 0.0, shift_cols(west, 1, 0))
@@ -124,19 +146,24 @@
             )
 
 
-def conv_call(block, top, bot, up, down, kernels):
-    shape = (2, 2, COLS, WIDTH)
+def edge_call(block, *args):
+    return pl.pallas_call(
+        lambda *refs: edge_kernel(block, *refs),
+        out_shape=(pltpu.VMEM((4, WIDTH), F32), pltpu.VMEM((4, WIDTH), F32)),
+        in_specs=[VM] * len(args),
+        out_specs=(VM, VM),
+        compiler_params=PARAMS,
+    )(*near(*args))
+
+
+def conv_call(block, *args):
     return pl.pallas_call(
         lambda *refs: conv_kernel(block, *refs),
-        out_shape=(
-            pltpu.VMEM(shape, F32),
-            pltpu.VMEM((4, WIDTH), F32),
-            pltpu.VMEM((4, WIDTH), F32),
-        ),
+        out_shape=pltpu.VMEM((2, 2, COLS, WIDTH), F32),
         in_specs=[VM] * 5,
-        out_specs=(VM,) * 3,
-        compiler_params=PARAMS,
-    )(*near(top, bot, up, down, kernels))
+        out_specs=VM,
+        compiler_params=PARAMS,
+    )(*near(*args))
 
 
 def block_body(block, scale_ref, part_ref, mate_ref, far_ref, mask_ref, gain_ref, mlp_gain_ref,
@@ -281,29 +308,28 @@
     )(*near(*args))
 
 
-def taps3(field, k_ref, index):
-    zero = jnp.zeros_like(field[:1])
-    above = jnp.concatenate([zero, field[:-1]], axis=0)
-    below = jnp.concatenate([field[1:], zero], axis=0)
-
-    def column(j):
-        return (
+def taps3(columns, k_ref, index):
+    total = 0.0
+    for j, field in enumerate(columns):
+        zero = jnp.zeros_like(field[:1])
+        above = jnp.concatenate([zero, field[:-1]], axis=0)
+        below = jnp.concatenate([field[1:], zero], axis=0)
+        total = total + (
             k_ref[index, 0, j : j + 1, :] * above
             + k_ref[index, 1, j : j + 1, :] * field
             + k_ref[index, 2, j : j + 1, :] * below
         )
-
-    return column(1) + shift_cols(column(0), 1, 1) + shift_cols(column(2), -1, 1)
+    return total
 
 
 def ocean_kernel(scale_ref, own_ref, pair_ref, next_ref, k_ref, point_ref, gain_ref, qkv_ref,
-                 out_ref, last_ref, pool_ref, wide_ref):
+                 out_ref, last_ref, field_ref, pool_ref, wide_ref, merged_ref):
     mean_matrix = head_mean(128)
     row = lax.broadcasted_iota(jnp.int32, (128, 128), 0) % 8
     col = lax.broadcasted_iota(jnp.int32, (128, 128), 1) % 8
     mask = jnp.where(row == col, 1.0, 0.0)
-    wide_ref[...] = jnp.zeros_like(wide_ref)
     first_of_pair = (lax.axis_index("lat") + lax.axis_index("comp")) % 2 == 0
+    fine_all = []
     for m in range(2):
         def rows_of(ref):
             even = ref[:, 2 * m].astype(F32)[:, None]
@@ -312,40 +338,52 @@
 
         pair = rows_of(pair_ref)
         following = rows_of(next_ref)
-        west = jnp.where(first_of_pair, following, pair)
-        east = jnp.where(first_of_pair, pair, following)
-        field = jnp.concatenate([west, rows_of(own_ref), east], axis=1)
-        act = taps3(field, k_ref, 0).astype(BF16).reshape(32 * 24, OCEAN)
-        fine = gelu(dot(act, point_ref[0])).astype(BF16).astype(F32)
-        fine4 = fine.reshape(16, 2, 24, OCEAN)
-        pool_ref[...] = (fine4[:, 0] + fine4[:, 1]).reshape(16 * 24, OCEAN)
-        coarse = []
-        for i in range(16):
-            coarse.append(
-                pool_ref[pl.ds(24 * i + 4, 8, stride=2), :]
-                + pool_ref[pl.ds(24 * i + 5, 8, stride=2), :]
+        field_ref[m, :, 0:8, :] = jnp.where(first_of_pair, following, pair)
+        field_ref[m, :, 8:16, :] = rows_of(own_ref)
+        field_ref[m, :, 16:24, :] = jnp.where(first_of_pair, pair, following)
+        act = taps3([field_ref[m, :, 3 + j : 19 + j, :] for j in range(3)], k_ref, 0)
+        act = act.astype(BF16).reshape(32 * 16, OCEAN)
+        fine = gelu(dot(act, point_ref[0])).astype(BF16).astype(F32).reshape(16, 2, 16, OCEAN)
+        fine_all.append(fine)
+        pool_ref[m] = (fine[:, 0] + fine[:, 1]).reshape(256, OCEAN)
+    coarse = []
+    for m in range(2):
+        pooled = pool_ref[m, pl.ds(0, 128, stride=2), :] + pool_ref[m, pl.ds(1, 128, stride=2), :]
+        coarse.append((pooled * 0.25).astype(BF16).astype(F32).reshape(16, 8, OCEAN))
+    acts = []
+    for m in range(2):
+        columns = (shift_cols(coarse[m], 1, 1), coarse[m], shift_cols(coarse[m], -1, 1))
+        acts.append(taps3(columns, k_ref, 1).astype(BF16).reshape(128, OCEAN))
+    first = gelu(dot(jnp.concatenate(acts, axis=0), point_ref[1])).astype(BF16).astype(F32)
+    normed = norm_rows(first, gain_ref[...]).astype(BF16)
+    qkv = dot(normed, qkv_ref[...])
+    query = unit(qkv[:, :128], mean_matrix)
+    key = unit(qkv[:, 128:256], mean_matrix)
+    value = qkv[:, 256:].astype(BF16)
+    attended = []
+    for m in range(2):
+        at = slice(128 * m, 128 * m + 128)
+        attended.append(
+            pair_attend(
+                query[at],
+                key[at],
+                value[at],
+                mask,
+                scale_ref[:, 0:1] * (LOG2E / 64),
+                scale_ref[:, 1:2] * (LOG2E / 64),
             )
-        coarse = (jnp.concatenate(coarse, axis=0) * 0.25).astype(BF16).astype(F32)
-        act = taps3(coarse.reshape(16, 8, OCEAN), k_ref, 1).astype(BF16).reshape(128, OCEAN)
-        first = gelu(dot(act, point_ref[1])).astype(BF16).astype(F32)
-        normed = norm_rows(first, gain_ref[...]).astype(BF16)
-        qkv = dot(normed, qkv_ref[...])
-        attended = pair_attend(
-            unit(qkv[:, :128], mean_matrix),
-            unit(qkv[:, 128:256], mean_matrix),
-            qkv[:, 256:].astype(BF16),
-            mask,
-            scale_ref[:, 0:1] * (LOG2E / 64),
-            scale_ref[:, 1:2] * (LOG2E / 64),
         )
-        following = (first + dot(attended, out_ref[...])).astype(BF16).astype(F32)
-        for i in range(16):
-            piece = following[8 * i : 8 * i + 8]
-            wide_ref[pl.ds(24 * i + 4, 8, stride=2), :] = piece
-            wide_ref[pl.ds(24 * i + 5, 8, stride=2), :] = piece
-        spread = wide_ref[...].reshape(16, 1, 24, OCEAN)
-        merged = (fine4 + spread).astype(BF16).astype(F32).reshape(32, 24, OCEAN)
-        act = taps3(merged, k_ref, 2)[:, 8:16].astype(BF16).reshape(16, 2, 8, OCEAN)
+    attended = jnp.concatenate(attended, axis=0)
+    coarse_next = (first + dot(attended, out_ref[...])).astype(BF16).astype(F32)
+    for m in range(2):
+        piece = coarse_next[128 * m : 128 * m + 128]
+        wide_ref[m, pl.ds(0, 128, stride=2), :] = piece
+        wide_ref[m, pl.ds(1, 128, stride=2), :] = piece
+    for m in range(2):
+        spread = wide_ref[m].reshape(16, 1, 16, OCEAN)
+        merged_ref[m] = (fine_all[m] + spread).astype(BF16).astype(F32).reshape(32, 16, OCEAN)
+        act = taps3([merged_ref[m, :, 3 + j : 11 + j, :] for j in range(3)], k_ref, 2)
+        act = act.astype(BF16).reshape(16, 2, 8, OCEAN)
         last_ref[:, 2 * m] = act[:, 0]
         last_ref[:, 2 * m + 1] = act[:, 1]
 
@@ -357,7 +395,12 @@
         in_specs=[VM] * 9,
         out_specs=VM,
         compiler_params=PARAMS,
-        scratch_shapes=[pltpu.VMEM((16 * 24, OCEAN), F32), pltpu.VMEM((16 * 24, OCEAN), F32)],
+        scratch_shapes=[
+            pltpu.VMEM((2, 32, 24, OCEAN), F32),
+            pltpu.VMEM((2, 256, OCEAN), F32),
+            pltpu.VMEM((2, 256, OCEAN), F32),
+            pltpu.VMEM((2, 32, 16, OCEAN), F32),
+        ],
         name="ocean",
     )(*near(*args))
 
@@ -365,22 +408,29 @@
 def final_kernel(last_ref, start_ref, cur_ref, sea_ref, point_ref, return_ref, air_hbm, water_hbm,
                  air_ref, water_ref, sems):
     copies = []
+
+    def send(src, dst, m, r, k):
+        copies.append(pltpu.make_async_copy(src.at[m, r], dst.at[m, r], sems.at[k]))
+        copies[-1].start()
+
     straight = lax.axis_index("comp") == 0
-    for m in range(2):
-        for r in range(2):
-            i = 2 * m + r
-            act = turned(last_ref[:, i].astype(F32), straight).astype(BF16).reshape(COLS, OCEAN)
-            start = turned(start_ref[:, i].astype(F32), straight).reshape(COLS, OCEAN)
-            lifted = gelu(dot(act, point_ref[2]))
-            sea = sea_ref[r]
-            water = (sea * (start + lifted)).astype(BF16)
-            water_ref[m, r] = water
-            back = dot(water, return_ref[...])
-            sea3 = jnp.concatenate([sea, sea, sea], axis=1)
-            air_ref[m, r] = (cur_ref[m, r].astype(F32) + sea3 * back).astype(BF16)
-            for k, (src, dst) in enumerate(((water_ref, water_hbm), (air_ref, air_hbm))):
-                copies.append(pltpu.make_async_copy(src.at[m, r], dst.at[m, r], sems.at[2 * i + k]))
-                copies[-1].start()
+    acts = [
+        turned(last_ref[:, i].astype(F32), straight).astype(BF16).reshape(COLS, OCEAN) for i in range(4)
+    ]
+    lifted = gelu(dot(jnp.concatenate(acts, axis=0), point_ref[2]))
+    waters = []
+    for i in range(4):
+        m, r = i // 2, i % 2
+        start = turned(start_ref[:, i].astype(F32), straight).reshape(COLS, OCEAN)
+        waters.append((sea_ref[r] * (start + lifted[COLS * i : COLS * i + COLS])).astype(BF16))
+        water_ref[m, r] = waters[i]
+        send(water_ref, water_hbm, m, r, i)
+    back = dot(jnp.concatenate(waters, axis=0), return_ref[...])
+    for i in range(4):
+        m, r = i // 2, i % 2
+        sea = jnp.concatenate([sea_ref[r]] * 3, axis=1)
+        air_ref[m, r] = (cur_ref[m, r].astype(F32) + sea * back[COLS * i : COLS * i + COLS]).astype(BF16)
+        send(air_ref, air_hbm, m, r, 4 + i)
     for copy in copies:
         copy.wait()
 
@@ -428,14 +478,15 @@
     return sorted(pairs)
 
 
-def mix(block, top, bot, kernels):
+def mix(block, top, bot, kernels, *after):
     lats = lax.axis_size("lat")
     sectors = lax.axis_size("lon") * lax.axis_size("comp")
     up = lax.ppermute(bot, "lat", ring(lats, 1))
     down = lax.ppermute(top, "lat", ring(lats, -1))
-    part, mate, far = conv_call(block, top, bot, up, down, kernels)
+    mate, far = edge_call(block, top, bot, up, down, kernels, *after)
     far = lax.ppermute(far, LON, [(i, (i + 2 * (i % 2) - 1) % sectors) for i in range(sectors)])
     mate = lax.ppermute(mate, LON, [(i, i ^ 1) for i in range(sectors)])
+    part = conv_call(block, top, bot, up, down, kernels)
     return part, mate, far
 
 
@@ -506,7 +557,7 @@
         1, ocean_prev, flux_matrix, conv_ocean, point_matrix, ocean_gain[None, :], ocean_qkv,
         ocean_scale[None, :], ocean_out, seaside_return_matrix, *big
     )
-    part, mate, far = mix(1, top, bot, conv_atm)
+    part, mate, far = mix(1, top, bot, conv_atm, ocean_scale)
     current, start = second_call(
         attn_scales, part, mate, far, mask, *small, *weights, ocean_prev, sea, flux_matrix
     )

time: 85.6 us -> 82.7 us (0.966)
  waiting for transfers between devices: 16.1 us -> 14.4 us
  Pallas kernels: 19.3 us -> 17.8 us
    ppermute x2, waiting for transfers between devices: 5.24 us -> 2.8 us  [mix(): down = lax.ppermute(top, 'lat', ring(lats, -1))]
    pallas_call x1, Pallas kernels: 2.99 us -> 1.84 us  [ocean_call(): pl.pallas_call(ocean_kernel, out_shape=pltpu.VMEM((16, 4, 8, OCEAN), BF16...]
  transfers between devices with their start and end apart: 10 -> 10, of which waited for: 7 -> 8; matrix products, arithmetic and copies ran while one was open for 0% -> 0% of each run, Pallas kernels for 5% -> 7%
where the time goes in v1:
time: 82.7 us; the launch traced here: 82.5 us
  blocking collectives  28.5 us (34%)
  starting transfers between devices  19.9 us (24%)
  Pallas kernels  17.8 us (22%)
  waiting for transfers between devices  14.4 us (17%)
  local copies, waits for them, and re-layouts  1.07 us (1%)
  between operations  0.88 us (1%)
    all_to_all x1, blocking collectives, per_device(): own = lax.all_to_all(start, 'lat', 0, 0)  15.6 us
    all_to_all x1, blocking collectives, per_device(): last = lax.all_to_all(last, 'lat', 0, 0)  12.8 us
    ppermute x2, starting transfers between devices, mix(): lax.ppermute(far, LON, [(i, (i + 2 * (i % 2) - 1) % sectors) for i in ran...  10.3 us
    ppermute x2, waiting for transfers between devices, mix(): up = lax.ppermute(bot, 'lat', ring(lats, 1))  6.53 us
    pallas_call x2, Pallas kernels, load_call(): pl.pallas_call(lambda *refs: load_kernel(block, count, *refs), out_shape=...  4.64 us
    pallas_call x1, Pallas kernels, second_call(): pl.pallas_call(second_kernel, out_shape=(pltpu.VMEM((2, 2, COLS, WIDTH),...  4.45 us
    pallas_call x1, Pallas kernels, first_call(): pl.pallas_call(first_kernel, out_shape=(row, row), in_specs=[VM] * 13, ou...  4.33 us
    ppermute x2, starting transfers between devices, mix(): down = lax.ppermute(top, 'lat', ring(lats, -1))  3.53 us
  transfers between devices with their start and end apart: 10, of which 8 were waited for; matrix products, arithmetic and copies ran while one was open for 0% of the time, Pallas kernels for 7%

profile of v1, /device:TPU:32, one launch (start us, length us, event | category | flops | bytes accessed | tf_op | source)
XLA Modules:
  0.0 82.5 jit_solution(8374370950139521324)
XLA Ops:
  0.6 1.1 %slice_bitcast_fusion = (bf16[2,128,384]{2,1,0:T(8,128)(2,1)S(1)}, bf16[2,128,384]{2,1,0:T(8,128)(2,1)S(1)}) fusion(bf16[2,2,128,384]{3,2,1,0:T(8,128)(2,1)} %param.22), kind=kLoop, calls=%fused_computation | loop fusion | bytes 786432 | tf_op jit(solution)/shard_map/squeeze | solution.py:552
  1.7 2.0 %collective-permute-start = (bf16[2,128,384]{2,1,0:T(8,128)(2,1)S(1)}, bf16[2,128,384]{2,1,0:T(8,128)(2,1)S(1)}, u32[]{:S(2)}, u32[]{:S(2)}) collective-permute-start(bf16[2,128,384]{2,1,0:T(8,128)(2,1)S(1)} %get-tuple-element.68.refs_1_), channel_id=1, source_target_pairs={{0,16},{16,32},{32,48},{48,64},{64,80},{80,96},{96,112},{112,128},... | collective-permute-start | bytes 589832 | tf_op jit(solution)/shard_map/ppermute | solution.py:484
  3.7 0.1 collective-permute-start.1
  3.8 2.2 %shard_map.222 = (f32[2,128,128]{2,1,0:T(8,128)S(1)}, f32[2,128,128]{2,1,0:T(8,128)S(1)}, f32[3,3,2,384]{3,2,1,0:T(2,128)S(1)}, f32[2,6]{1,0:T(2,128)S(1)}, f32[...) custom-call(s32[2,128]{1,0:T(2,128)} %refs_0_.3, ...), custom_call_target="tpu_custom_call" | custom-call | tf_op jit(solution)/shard_map/pallas_call | solution.py:532
  6.0 2.4 %collective-permute-done.refs_2_ = bf16[2,128,384]{2,1,0:T(8,128)(2,1)S(1)} collective-permute-done((bf16[2,128,384]{2,1,0:T(8,128)(2,1)S(1)}, bf16[2,128,384]{2,1,0:T(8,128)(2,1)S(1)}, u32[]{:S(2)}, u32[]{:S(2)}) %collective-permute-start) | collective-permute-done | bytes 196640 | tf_op jit(solution)/shard_map/ppermute | solution.py:484
  8.4 1.8 %collective-permute-done.1.refs_3_ = bf16[2,128,384]{2,1,0:T(8,128)(2,1)S(1)} collective-permute-done((bf16[2,128,384]{2,1,0:T(8,128)(2,1)S(1)}, bf16[2,128,384]{2,1,0:T(8,128)(2,1)S(1)}, u32[]{:S(2)}, u32[]{:S(2)}) %collective-permute-start.1) | collective-permute-done | bytes 196640 | tf_op jit(solution)/shard_map/ppermute | solution.py:485
  10.3 0.1 collective-permute-start.2
  10.4 5.5 %collective-permute-start.3 = (f32[4,384]{1,0:T(4,128)S(1)}, f32[4,384]{1,0:T(4,128)S(1)}, u32[]{:S(2)}, u32[]{:S(2)}) collective-permute-start(f32[4,384]{1,0:T(4,128)S(1)} %get-tuple-element.39), channel_id=1, source_target_pairs={{0,15},{1,2},{2,1},{3,4},{4,3},{5,6},{6,5},{7,8},{8,7},{9,10},{10,... | collective-permute-start | bytes 18440 | tf_op jit(solution)/shard_map/ppermute | solution.py:487
  15.9 0.7 shard_map.223.part_ref
  16.5 0.0 collective-permute-done.2.mate_ref
  16.6 0.7 collective-permute-done.3.far_ref
  17.2 4.3 %block_0.1 = (bf16[2,128,384]{2,1,0:T(8,128)(2,1)S(1)}, bf16[2,128,384]{2,1,0:T(8,128)(2,1)S(1)}) custom-call(f32[2,6]{1,0:T(2,128)S(1)} %get-tuple-element.36.scale_ref, f32[2,2,128,384]{3,2,1,0:T(8,128)S(1)} %shard_map.223.part_ref, f32[4,384]{1,0:T(4,128)S(1)} %collective-permute-done.2.mate_ref, f32[4,384]{1,0:T(4,128)S(1)} %collective-permute-done.3.far_ref, ...), custom_call_target="tpu_custom_call" | custom-call | tf_op jit(solution)/shard_map/block_0/pallas_call | solution.py:287
  21.5 3.4 %collective-permute-start.5 = (bf16[2,128,384]{2,1,0:T(8,128)(2,1)S(1)}, bf16[2,128,384]{2,1,0:T(8,128)(2,1)S(1)}, u32[]{:S(2)}, u32[]{:S(2)}) collective-permute-start(bf16[2,128,384]{2,1,0:T(8,128)(2,1)S(1)} %get-tuple-element.49.refs_0_), channel_id=1, source_target_pairs={{0,240},{16,0},{32,16},{48,32},{64,48},{80,64},{96,80},{112,96},{1... | collective-permute-start | bytes 589832 | tf_op jit(solution)/shard_map/ppermute | solution.py:485
  25.0 0.0 collective-permute-start.4
  25.0 2.4 %shard_map.221 = (bf16[2,2,128,128]{3,2,1,0:T(8,128)(2,1)S(1)}, bf16[384,128]{1,0:T(8,128)(2,1)S(1)}, f32[3,3,3,128]{3,2,1,0:T(4,128)S(1)}, bf16[3,128,128]{2,1,...) custom-call(bf16[2,2,128,128]{3,2,1,0:T(8,128)(2,1)} %refs_0_.2, ...), custom_call_target="tpu_custom_call" | custom-call | tf_op jit(solution)/shard_map/pallas_call | solution.py:532
  27.4 1.0 %collective-permute-done.5.refs_3_ = bf16[2,128,384]{2,1,0:T(8,128)(2,1)S(1)} collective-permute-done((bf16[2,128,384]{2,1,0:T(8,128)(2,1)S(1)}, bf16[2,128,384]{2,1,0:T(8,128)(2,1)S(1)}, u32[]{:S(2)}, u32[]{:S(2)}) %collective-permute-start.5) | collective-permute-done | bytes 196640 | tf_op jit(solution)/shard_map/ppermute | solution.py:485
  28.4 4.1 %collective-permute-done.4.refs_2_ = bf16[2,128,384]{2,1,0:T(8,128)(2,1)S(1)} collective-permute-done((bf16[2,128,384]{2,1,0:T(8,128)(2,1)S(1)}, bf16[2,128,384]{2,1,0:T(8,128)(2,1)S(1)}, u32[]{:S(2)}, u32[]{:S(2)}) %collective-permute-start.4) | collective-permute-done | bytes 196640 | tf_op jit(solution)/shard_map/ppermute | solution.py:484
  32.6 0.1 collective-permute-start.6
  32.7 4.8 %collective-permute-start.7 = (f32[4,384]{1,0:T(4,128)S(1)}, f32[4,384]{1,0:T(4,128)S(1)}, u32[]{:S(2)}, u32[]{:S(2)}) collective-permute-start(f32[4,384]{1,0:T(4,128)S(1)} %get-tuple-element.52), channel_id=1, source_target_pairs={{0,15},{1,2},{2,1},{3,4},{4,3},{5,6},{6,5},{7,8},{8,7},{9,10},{10,... | collective-permute-start | bytes 18440 | tf_op jit(solution)/shard_map/ppermute | solution.py:487
  37.5 0.7 shard_map.225.part_ref
  38.2 0.0 collective-permute-done.6.mate_ref
  38.2 1.5 %collective-permute-done.7.far_ref = f32[4,384]{1,0:T(4,128)S(1)} collective-permute-done((f32[4,384]{1,0:T(4,128)S(1)}, f32[4,384]{1,0:T(4,128)S(1)}, u32[]{:S(2)}, u32[]{:S(2)}) %collective-permute-start.7) | collective-permute-done | bytes 6176 | tf_op jit(solution)/shard_map/ppermute | solution.py:487
  39.6 4.4 %block_1.1 = (bf16[2,2,128,384]{3,2,1,0:T(8,128)(2,1)S(1)}, bf16[16,4,8,128]{3,2,1,0:T(8,128)(2,1)S(1)}) custom-call(f32[2,6]{1,0:T(2,128)S(1)} %get-tuple-element.36.scale_ref, f32[2,2,128,384]{3,2,1,0:T(8,128)S(1)} %shard_map.225.part_ref, f32[4,384]{1,0:T(4,128)S(1)} %collective-permute-done.6.mate_ref, f32[4,384]{1,0:T(4,128)S(1)} %collective-permute-done.7.far_ref, ...), custom_call_target="tpu_custom_call" | custom-call | tf_op jit(solution)/shard_map/block_1/pallas_call | solution.py:298
  44.1 15.6 %all_to_all.10.own_ref = bf16[16,4,8,128]{3,2,1,0:T(8,128)(2,1)S(1)} all-to-all(bf16[16,4,8,128]{3,2,1,0:T(8,128)(2,1)S(1)} %get-tuple-element.60.start_ref), channel_id=1, replica_groups=mesh['lat'=16,'lon'=8,'comp'=2] {'lat'}, dimensions={0} | all-to-all | bytes 262144 | tf_op jit(solution)/shard_map/all_to_all | solution.py:564
  59.7 0.7 collective-permute-start.9
  60.4 3.2 %collective-permute-start.8 = (bf16[16,4,8,128]{3,2,1,0:T(8,128)(2,1)S(1)}, bf16[16,4,8,128]{3,2,1,0:T(8,128)(2,1)S(1)}, u32[]{:S(2)}, u32[]{:S(2)}) collective-permute-start(bf16[16,4,8,128]{3,2,1,0:T(8,128)(2,1)S(1)} %all_to_all.10.own_ref), channel_id=1, source_target_pairs={{0,16},{1,17},{2,18},{3,19},{4,20},{5,21},{6,22},{7,23},{8,24},{9,... | collective-permute-start | bytes 393224 | tf_op jit(solution)/shard_map/ppermute | solution.py:566
  63.6 1.0 %collective-permute-done.9.next_ref = bf16[16,4,8,128]{3,2,1,0:T(8,128)(2,1)S(1)} collective-permute-done((bf16[16,4,8,128]{3,2,1,0:T(8,128)(2,1)S(1)}, bf16[16,4,8,128]{3,2,1,0:T(8,128)(2,1)S(1)}, u32[]{:S(2)}, u32[]{:S(2)}) %collective-permute-start.9) | collective-permute-done | bytes 131104 | tf_op jit(solution)/shard_map/ppermute | solution.py:567
  64.7 1.9 %collective-permute-done.8.pair_ref = bf16[16,4,8,128]{3,2,1,0:T(8,128)(2,1)S(1)} collective-permute-done((bf16[16,4,8,128]{3,2,1,0:T(8,128)(2,1)S(1)}, bf16[16,4,8,128]{3,2,1,0:T(8,128)(2,1)S(1)}, u32[]{:S(2)}, u32[]{:S(2)}) %collective-permute-start.8) | collective-permute-done | bytes 131104 | tf_op jit(solution)/shard_map/ppermute | solution.py:566
  66.6 1.8 %ocean.1 = bf16[16,4,8,128]{3,2,1,0:T(8,128)(2,1)S(1)} custom-call(f32[1,2]{1,0:T(1,128)S(1)} %get-tuple-element.35.refs_5_.scale_ref, bf16[16,4,8,128]{3,2,1,0:T(8,128)(2,1)S(1)} %all_to_all.10.own_ref, bf16[16,4,8,128]{3,2,1,0:T(8,128)(2,1)S(1)} %collective-permute-done.8.pair_ref, bf16[16,4,8,128]{3,2,1,0:T(8,128)(2,1)S(1)} %collective-permute-done.9.next_ref, ...), custom_call_target="tpu_custom_call" | custom-call | tf_op jit(solution)/shard_map/ocean/pallas_call | solution.py:392
  68.4 12.8 %all_to_all.11.last_ref = bf16[16,4,8,128]{3,2,1,0:T(8,128)(2,1)S(1)} all-to-all(bf16[16,4,8,128]{3,2,1,0:T(8,128)(2,1)S(1)} %ocean.1), channel_id=1, replica_groups=mesh['lat'=16,'lon'=8,'comp'=2] {'lat'}, dimensions={0} | all-to-all | bytes 262144 | tf_op jit(solution)/shard_map/all_to_all | solution.py:570
  81.3 1.1 %final.1 = (bf16[2,2,128,384]{3,2,1,0:T(8,128)(2,1)}, bf16[2,2,128,128]{3,2,1,0:T(8,128)(2,1)}) custom-call(bf16[16,4,8,128]{3,2,1,0:T(8,128)(2,1)S(1)} %all_to_all.11.last_ref, bf16[16,4,8,128]{3,2,1,0:T(8,128)(2,1)S(1)} %get-tuple-element.60.start_ref, bf16[2,2,128,384]{3,2,1,0:T(8,128)(2,1)S(1)} %get-tuple-element.66.cur_ref, ...), custom_call_target="tpu_custom_call" | custom-call | tf_op jit(solution)/shard_map/final/pallas_call | solution.py:439
  (2 shorter events, 0.1 us)
Async XLA Ops:
  1.7 6.7 %collective-permute-start = (bf16[2,128,384]{2,1,0:T(8,128)(2,1)S(1)}, bf16[2,128,384]{2,1,0:T(8,128)(2,1)S(1)}, u32[]{:S(2)}, u32[]{:S(2)}) collective-permute-start(bf16[2,128,384]{2,1,0:T(8,128)(2,1)S(1)} %get-tuple-element.68.refs_1_), channel_id=1, source_target_pairs={{0,16},{16,32},{32,48},{48,64},{64,80},{80,96},{96,112},{112,128},... | collective-permute-start | bytes 589832 | tf_op jit(solution)/shard_map/ppermute | solution.py:484
  3.7 6.5 %collective-permute-start.1 = (bf16[2,128,384]{2,1,0:T(8,128)(2,1)S(1)}, bf16[2,128,384]{2,1,0:T(8,128)(2,1)S(1)}, u32[]{:S(2)}, u32[]{:S(2)}) collective-permute-start(bf16[2,128,384]{2,1,0:T(8,128)(2,1)S(1)} %get-tuple-element.69.refs_0_), channel_id=1, source_target_pairs={{0,240},{16,0},{32,16},{48,32},{64,48},{80,64},{96,80},{112,96},{1... | collective-permute-start | bytes 589832 | tf_op jit(solution)/shard_map/ppermute | solution.py:485
  10.3 6.3 %collective-permute-start.2 = (f32[4,384]{1,0:T(4,128)S(1)}, f32[4,384]{1,0:T(4,128)S(1)}, u32[]{:S(2)}, u32[]{:S(2)}) collective-permute-start(f32[4,384]{1,0:T(4,128)S(1)} %get-tuple-element.38), channel_id=1, source_target_pairs={{0,1},{1,0},{2,3},{3,2},{4,5},{5,4},{6,7},{7,6},{8,9},{9,8},{10,11... | collective-permute-start | bytes 18440 | tf_op jit(solution)/shard_map/ppermute | solution.py:488
  10.4 6.8 %collective-permute-start.3 = (f32[4,384]{1,0:T(4,128)S(1)}, f32[4,384]{1,0:T(4,128)S(1)}, u32[]{:S(2)}, u32[]{:S(2)}) collective-permute-start(f32[4,384]{1,0:T(4,128)S(1)} %get-tuple-element.39), channel_id=1, source_target_pairs={{0,15},{1,2},{2,1},{3,4},{4,3},{5,6},{6,5},{7,8},{8,7},{9,10},{10,... | collective-permute-start | bytes 18440 | tf_op jit(solution)/shard_map/ppermute | solution.py:487
  21.5 6.9 %collective-permute-start.5 = (bf16[2,128,384]{2,1,0:T(8,128)(2,1)S(1)}, bf16[2,128,384]{2,1,0:T(8,128)(2,1)S(1)}, u32[]{:S(2)}, u32[]{:S(2)}) collective-permute-start(bf16[2,128,384]{2,1,0:T(8,128)(2,1)S(1)} %get-tuple-element.49.refs_0_), channel_id=1, source_target_pairs={{0,240},{16,0},{32,16},{48,32},{64,48},{80,64},{96,80},{112,96},{1... | collective-permute-start | bytes 589832 | tf_op jit(solution)/shard_map/ppermute | solution.py:485
  25.0 7.6 %collective-permute-start.4 = (bf16[2,128,384]{2,1,0:T(8,128)(2,1)S(1)}, bf16[2,128,384]{2,1,0:T(8,128)(2,1)S(1)}, u32[]{:S(2)}, u32[]{:S(2)}) collective-permute-start(bf16[2,128,384]{2,1,0:T(8,128)(2,1)S(1)} %get-tuple-element.50.refs_1_), channel_id=1, source_target_pairs={{0,16},{16,32},{32,48},{48,64},{64,80},{80,96},{96,112},{112,128},... | collective-permute-start | bytes 589832 | tf_op jit(solution)/shard_map/ppermute | solution.py:484
  32.6 5.6 %collective-permute-start.6 = (f32[4,384]{1,0:T(4,128)S(1)}, f32[4,384]{1,0:T(4,128)S(1)}, u32[]{:S(2)}, u32[]{:S(2)}) collective-permute-start(f32[4,384]{1,0:T(4,128)S(1)} %get-tuple-element.51), channel_id=1, source_target_pairs={{0,1},{1,0},{2,3},{3,2},{4,5},{5,4},{6,7},{7,6},{8,9},{9,8},{10,11... | collective-permute-start | bytes 18440 | tf_op jit(solution)/shard_map/ppermute | solution.py:488
  32.7 6.9 %collective-permute-start.7 = (f32[4,384]{1,0:T(4,128)S(1)}, f32[4,384]{1,0:T(4,128)S(1)}, u32[]{:S(2)}, u32[]{:S(2)}) collective-permute-start(f32[4,384]{1,0:T(4,128)S(1)} %get-tuple-element.52), channel_id=1, source_target_pairs={{0,15},{1,2},{2,1},{3,4},{4,3},{5,6},{6,5},{7,8},{8,7},{9,10},{10,... | collective-permute-start | bytes 18440 | tf_op jit(solution)/shard_map/ppermute | solution.py:487
  59.7 5.0 %collective-permute-start.9 = (bf16[16,4,8,128]{3,2,1,0:T(8,128)(2,1)S(1)}, bf16[16,4,8,128]{3,2,1,0:T(8,128)(2,1)S(1)}, u32[]{:S(2)}, u32[]{:S(2)}) collective-permute-start(bf16[16,4,8,128]{3,2,1,0:T(8,128)(2,1)S(1)} %all_to_all.10.own_ref), channel_id=1, source_target_pairs={{0,15},{1,2},{2,1},{3,4},{4,3},{5,6},{6,5},{7,8},{8,7},{9,10},{10,... | collective-permute-start | bytes 393224 | tf_op jit(solution)/shard_map/ppermute | solution.py:567
  60.4 6.1 %collective-permute-start.8 = (bf16[16,4,8,128]{3,2,1,0:T(8,128)(2,1)S(1)}, bf16[16,4,8,128]{3,2,1,0:T(8,128)(2,1)S(1)}, u32[]{:S(2)}, u32[]{:S(2)}) collective-permute-start(bf16[16,4,8,128]{3,2,1,0:T(8,128)(2,1)S(1)} %all_to_all.10.own_ref), channel_id=1, source_target_pairs={{0,16},{1,17},{2,18},{3,19},{4,20},{5,21},{6,22},{7,23},{8,24},{9,... | collective-permute-start | bytes 393224 | tf_op jit(solution)/shard_map/ppermute | solution.py:566

commit v2 on v1

--- a/solution.py
+++ b/solution.py
@@ -119,7 +119,15 @@
     return (lat > 0).astype(F32), (lat < lax.axis_size("lat") - 1).astype(F32)
 
 
-def conv_kernel(block, top_ref, bot_ref, up_ref, down_ref, k_ref, part_ref):
+def project(mixed, gain, qkv):
+    mean_matrix = head_mean(256)
+    out = dot(norm_rows(mixed, gain).astype(BF16), qkv)
+    units = [unit(out[:, 256 * i : 256 * i + 256], mean_matrix) for i in range(3)]
+    return jnp.concatenate(units + [out[:, 2 * WIDTH :].astype(BF16)], axis=1)
+
+
+def conv_kernel(block, top_ref, bot_ref, up_ref, down_ref, k_ref, gain_ref, qkv_ref, mixed_ref,
+                units_ref, ends_ref):
     has_up, has_down = inner_rows()
     first_col = lax.broadcasted_iota(jnp.int32, (COLS, WIDTH), 0) == 0
     final_col = lax.broadcasted_iota(jnp.int32, (COLS, WIDTH), 0) == COLS - 1
@@ -127,6 +135,7 @@
     def tap(i, j):
         return k_ref[i, j, block : block + 1, :]
 
+    parts = []
     for m in range(2):
         rows = [
             up_ref[m].astype(F32) * has_up,
@@ -139,11 +148,18 @@
             mid = tap(0, 1) * a + (tap(1, 1) + 1.0) * b + tap(2, 1) * c
             west = tap(0, 0) * a + tap(1, 0) * b + tap(2, 0) * c
             east = tap(0, 2) * a + tap(1, 2) * b + tap(2, 2) * c
-            part_ref[m, r] = (
+            part = (
                 mid
                 + jnp.where(first_col, 0.0, shift_cols(west, 1, 0))
                 + jnp.where(final_col, 0.0, shift_cols(east, -1, 0))
             )
+            i = 2 * m + r
+            ends_ref[i : i + 1, :] = part[:1]
+            ends_ref[4 + i : 5 + i, :] = part[COLS - 1 :]
+            parts.append(part.astype(BF16))
+    mixed = jnp.concatenate(parts, axis=0)
+    mixed_ref[...] = mixed
+    units_ref[...] = project(mixed.astype(F32), gain_ref[block : block + 1, :], qkv_ref[...])
 
 
 def edge_call(block, *args):
@@ -159,38 +175,38 @@
 def conv_call(block, *args):
     return pl.pallas_call(
         lambda *refs: conv_kernel(block, *refs),
-        out_shape=pltpu.VMEM((2, 2, COLS, WIDTH), F32),
-        in_specs=[VM] * 5,
-        out_specs=VM,
+        out_shape=(
+            pltpu.VMEM((4 * COLS, WIDTH), BF16),
+            pltpu.VMEM((4 * COLS, 3 * WIDTH), BF16),
+            pltpu.VMEM((8, WIDTH), F32),
+        ),
+        in_specs=[VM] * 7,
+        out_specs=(VM,) * 3,
         compiler_params=PARAMS,
     )(*near(*args))
 
 
-def block_body(block, scale_ref, part_ref, mate_ref, far_ref, mask_ref, gain_ref, mlp_gain_ref,
-               min_ref, mout_ref, weights, store):
+def patched(ref, ends, i):
+    at = lax.broadcasted_iota(jnp.int32, (16, ref.shape[1]), 0)
+    low = jnp.where(at == 0, ends[i : i + 1], ref[COLS * i : COLS * i + 16, :].astype(F32))
+    high = jnp.where(
+        at == 15, ends[4 + i : 5 + i], ref[COLS * i + 112 : COLS * i + 128, :].astype(F32)
+    )
+    middle = ref[COLS * i + 16 : COLS * i + 112, :]
+    return jnp.concatenate([low.astype(BF16), middle, high.astype(BF16)], axis=0)
+
+
+def block_body(block, scale_ref, mixed_ref, units_ref, ends_ref, mate_ref, far_ref, mask_ref, gain_ref,
+               mlp_gain_ref, min_ref, mout_ref, weights, store):
     qkv_ref, out_ref, up_ref, down_ref = weights
-    first_col = lax.broadcasted_iota(jnp.int32, (COLS, WIDTH), 0) == 0
-    final_col = lax.broadcasted_iota(jnp.int32, (COLS, WIDTH), 0) == COLS - 1
-    mean_matrix = head_mean(256)
     even = lax.axis_index("comp") == 0
-    rows = []
-    for m in range(2):
-        for r in range(2):
-            i = 2 * m + r
-            x = part_ref[m, r]
-            mate = mate_ref[i : i + 1, :]
-            far = far_ref[i : i + 1, :]
-            x = x + jnp.where(first_col, jnp.where(even, far, mate), 0.0)
-            x = x + jnp.where(final_col, jnp.where(even, mate, far), 0.0)
-            rows.append(x.astype(BF16))
-    mixed = jnp.concatenate(rows, axis=0).astype(F32)
-    normed = norm_rows(mixed, gain_ref[block : block + 1, :]).astype(BF16)
-    qkv = dot(normed, qkv_ref())
-    units = [unit(qkv[:, 256 * i : 256 * i + 256], mean_matrix) for i in range(3)]
-    value = qkv[:, 2 * WIDTH :].astype(BF16)
-
-    def lanes(j):
-        return units[j // 2][:, 128 * (j % 2) : 128 * (j % 2) + 128]
+    mate, far = mate_ref[...], far_ref[...]
+    first = ends_ref[:4] + jnp.where(even, far, mate)
+    final = ends_ref[4:] + jnp.where(even, mate, far)
+    ends = jnp.concatenate([first, final, first, final], axis=0).astype(BF16).astype(F32)
+    end_units = project(ends, gain_ref[block : block + 1, :], qkv_ref()).astype(F32)
+    units = [patched(units_ref, end_units, i) for i in range(4)]
+    mixed = jnp.concatenate([patched(mixed_ref, ends, i) for i in range(4)], axis=0).astype(F32)
 
     scales = [
         scale_ref[block : block + 1, h : h + 1] * (LOG2E / 64) for h in range(HEADS)
@@ -198,15 +214,14 @@
     row_out = []
     for first in range(0, 4, GROUP):
         cells = [(i, j) for i in range(first, first + GROUP) for j in range(3)]
-        spans = {i: slice(COLS * i, COLS * i + COLS) for i in range(first, first + GROUP)}
-        scores = [pair_scores(lanes(j)[spans[i]], lanes(3 + j)[spans[i]]) for i, j in cells]
+        lanes = [slice(128 * j, 128 * j + 128) for j in range(9)]
+        scores = [pair_scores(units[i][:, lanes[j]], units[i][:, lanes[3 + j]]) for i, j in cells]
         terms = [
             pair_terms(x, mask_ref[i % 2], scales[2 * j], scales[2 * j + 1])
             for x, (i, j) in zip(scores, cells)
         ]
         results = [
-            pair_result(t, value[spans[i], 128 * j : 128 * j + 128])
-            for t, (i, j) in zip(terms, cells)
+            pair_result(t, units[i][:, lanes[6 + j]]) for t, (i, j) in zip(terms, cells)
         ]
         for i in range(GROUP):
             row_out.append(jnp.concatenate(results[3 * i : 3 * i + 3], axis=1))
@@ -244,7 +259,7 @@
     )
 
 
-def first_kernel(scale_ref, part_ref, mate_ref, far_ref, mask_ref, gain_ref, mlp_gain_ref, min_ref,
+def first_kernel(scale_ref, mixed_ref, units_ref, ends_ref, mate_ref, far_ref, mask_ref, gain_ref, mlp_gain_ref, min_ref,
                  mout_ref, qkv_h, out_h, up_h, down_h, top_ref, bot_ref):
     weights = weight_getters((qkv_h, out_h, up_h, down_h))
 
@@ -253,7 +268,7 @@
             top_ref[m] = value[2 * m * COLS : (2 * m + 1) * COLS]
             bot_ref[m] = value[(2 * m + 1) * COLS : (2 * m + 2) * COLS]
 
-    block_body(0, scale_ref, part_ref, mate_ref, far_ref, mask_ref, gain_ref, mlp_gain_ref,
+    block_body(0, scale_ref, mixed_ref, units_ref, ends_ref, mate_ref, far_ref, mask_ref, gain_ref, mlp_gain_ref,
                min_ref, mout_ref, weights, store)
 
 
@@ -262,7 +277,7 @@
     return jnp.where(straight, value, back)
 
 
-def second_kernel(scale_ref, part_ref, mate_ref, far_ref, mask_ref, gain_ref, mlp_gain_ref, min_ref,
+def second_kernel(scale_ref, mixed_ref, units_ref, ends_ref, mate_ref, far_ref, mask_ref, gain_ref, mlp_gain_ref, min_ref,
                   mout_ref, qkv_h, out_h, up_h, down_h, prev_ref, sea_ref, flux_ref,
                   cur_ref, start_ref):
     weights = weight_getters((qkv_h, out_h, up_h, down_h))
@@ -278,7 +293,7 @@
             start = sea_ref[r] * (prev_ref[m, r].astype(F32) + flux[at])
             start_ref[:, i] = turned(start.reshape(16, 8, OCEAN), straight).astype(BF16)
 
-    block_body(1, scale_ref, part_ref, mate_ref, far_ref, mask_ref, gain_ref, mlp_gain_ref,
+    block_body(1, scale_ref, mixed_ref, units_ref, ends_ref, mate_ref, far_ref, mask_ref, gain_ref, mlp_gain_ref,
                min_ref, mout_ref, weights, store)
 
 
@@ -287,7 +302,7 @@
     return pl.pallas_call(
         first_kernel,
         out_shape=(row, row),
-        in_specs=[VM] * 13,
+        in_specs=[VM] * 15,
         out_specs=(VM, VM),
         compiler_params=PARAMS,
         name="block_0",
@@ -301,7 +316,7 @@
             pltpu.VMEM((2, 2, COLS, WIDTH), BF16),
             pltpu.VMEM((16, 4, 8, OCEAN), BF16),
         ),
-        in_specs=[VM] * 16,
+        in_specs=[VM] * 18,
         out_specs=(VM, VM),
         compiler_params=PARAMS,
         name="block_1",
@@ -478,7 +493,7 @@
     return sorted(pairs)
 
 
-def mix(block, top, bot, kernels, *after):
+def mix(block, top, bot, kernels, gain, qkv, *after):
     lats = lax.axis_size("lat")
     sectors = lax.axis_size("lon") * lax.axis_size("comp")
     up = lax.ppermute(bot, "lat", ring(lats, 1))
@@ -486,8 +501,8 @@
     mate, far = edge_call(block, top, bot, up, down, kernels, *after)
     far = lax.ppermute(far, LON, [(i, (i + 2 * (i % 2) - 1) % sectors) for i in range(sectors)])
     mate = lax.ppermute(mate, LON, [(i, i ^ 1) for i in range(sectors)])
-    part = conv_call(block, top, bot, up, down, kernels)
-    return part, mate, far
+    part = conv_call(block, top, bot, up, down, kernels, gain, qkv)
+    return (*part, mate, far)
 
 
 def start_copies(sources, targets, sems):
@@ -549,17 +564,17 @@
         mlp_gain, member_in, member_out, *big
     )
     small = (attn_gain, mlp_gain, member_in, member_out)
-    part, mate, far = mix(0, atm_state[:, 0], atm_state[:, 1], conv_atm)
-    top, bot = first_call(attn_scales, part, mate, far, mask, *small, *weights)
+    mixed = mix(0, atm_state[:, 0], atm_state[:, 1], conv_atm, attn_gain, weights[0])
+    top, bot = first_call(attn_scales, *mixed, mask, *small, *weights)
 
     (ocean_prev, flux_matrix, conv_ocean, point_matrix, ocean_gain, ocean_qkv, ocean_scale, ocean_out,
      seaside_return_matrix, *weights) = load_call(
         1, ocean_prev, flux_matrix, conv_ocean, point_matrix, ocean_gain[None, :], ocean_qkv,
         ocean_scale[None, :], ocean_out, seaside_return_matrix, *big
     )
-    part, mate, far = mix(1, top, bot, conv_atm, ocean_scale)
+    mixed = mix(1, top, bot, conv_atm, attn_gain, weights[0], ocean_scale)
     current, start = second_call(
-        attn_scales, part, mate, far, mask, *small, *weights, ocean_prev, sea, flux_matrix
+        attn_scales, *mixed, mask, *small, *weights, ocean_prev, sea, flux_matrix
     )
     own = lax.all_to_all(start, "lat", 0, 0)
     axes = ("lat",) + LON

time: 82.7 us -> 81.3 us (0.983)
  waiting for transfers between devices: 14.4 us -> 12 us
  Pallas kernels: 17.8 us -> 18.9 us
    ppermute x2, waiting for transfers between devices: 2.11 us -> 0.22 us  [mix(): lax.ppermute(far, LON, [(i, (i + 2 * (i % 2) - 1) % sectors) for i in ran...]
    pallas_call x3, Pallas kernels: 5.69 us -> 7.45 us  [the longest x2 3.81 us: conv_call(): pl.pallas_call(lambda *refs: conv_kernel(block, *refs), out_shape=(pltpu....]
  transfers between devices with their start and end apart: 10 -> 10, of which waited for: 8 -> 7; matrix products, arithmetic and copies ran while one was open for 0% -> 0% of each run, Pallas kernels for 7% -> 10%
where the time goes in v2:
time: 81.3 us; the launch traced here: 81.1 us
  blocking collectives  28.4 us (35%)
  starting transfers between devices  19.8 us (24%)
  Pallas kernels  18.9 us (23%)
  waiting for transfers between devices  12 us (15%)
  local copies, waits for them, and re-layouts  1.07 us (1%)
  between operations  0.89 us (1%)
    all_to_all x1, blocking collectives, per_device(): own = lax.all_to_all(start, 'lat', 0, 0)  15.6 us
    all_to_all x1, blocking collectives, per_device(): last = lax.all_to_all(last, 'lat', 0, 0)  12.8 us
    ppermute x2, starting transfers between devices, mix(): lax.ppermute(far, LON, [(i, (i + 2 * (i % 2) - 1) % sectors) for i in ran...  10.3 us
    ppermute x2, waiting for transfers between devices, mix(): up = lax.ppermute(bot, 'lat', ring(lats, 1))  5.93 us
    pallas_call x2, Pallas kernels, load_call(): pl.pallas_call(lambda *refs: load_kernel(block, count, *refs), out_shape=...  4.64 us
    pallas_call x2, Pallas kernels, conv_call(): pl.pallas_call(lambda *refs: conv_kernel(block, *refs), out_shape=(pltpu....  3.81 us
    pallas_call x1, Pallas kernels, second_call(): pl.pallas_call(second_kernel, out_shape=(pltpu.VMEM((2, 2, COLS, WIDTH),...  3.71 us
    pallas_call x1, Pallas kernels, first_call(): pl.pallas_call(first_kernel, out_shape=(row, row), in_specs=[VM] * 15, ou...  3.64 us
  transfers between devices with their start and end apart: 10, of which 7 were waited for; matrix products, arithmetic and copies ran while one was open for 0% of the time, Pallas kernels for 10%

profile of v2, /device:TPU:32, one launch (start us, length us, event | category | flops | bytes accessed | tf_op | source)
XLA Modules:
  0.0 81.1 jit_solution(1733165026465956772)
XLA Ops:
  0.6 1.1 %slice_bitcast_fusion = (bf16[2,128,384]{2,1,0:T(8,128)(2,1)S(1)}, bf16[2,128,384]{2,1,0:T(8,128)(2,1)S(1)}) fusion(bf16[2,2,128,384]{3,2,1,0:T(8,128)(2,1)} %param.22), kind=kLoop, calls=%fused_computation | loop fusion | bytes 786432 | tf_op jit(solution)/shard_map/squeeze | solution.py:567
  1.7 2.0 %collective-permute-start = (bf16[2,128,384]{2,1,0:T(8,128)(2,1)S(1)}, bf16[2,128,384]{2,1,0:T(8,128)(2,1)S(1)}, u32[]{:S(2)}, u32[]{:S(2)}) collective-permute-start(bf16[2,128,384]{2,1,0:T(8,128)(2,1)S(1)} %get-tuple-element.80.refs_1_), channel_id=1, source_target_pairs={{0,16},{16,32},{32,48},{48,64},{64,80},{80,96},{96,112},{112,128},... | collective-permute-start | bytes 589832 | tf_op jit(solution)/shard_map/ppermute | solution.py:499
  3.7 0.1 collective-permute-start.1
  3.8 2.2 %shard_map.222 = (f32[2,128,128]{2,1,0:T(8,128)S(1)}, f32[2,128,128]{2,1,0:T(8,128)S(1)}, f32[3,3,2,384]{3,2,1,0:T(2,128)S(1)}, f32[2,6]{1,0:T(2,128)S(1)}, f32[...) custom-call(s32[2,128]{1,0:T(2,128)} %refs_0_.3, ...), custom_call_target="tpu_custom_call" | custom-call | tf_op jit(solution)/shard_map/pallas_call | solution.py:547
  6.0 2.4 %collective-permute-done.refs_2_ = bf16[2,128,384]{2,1,0:T(8,128)(2,1)S(1)} collective-permute-done((bf16[2,128,384]{2,1,0:T(8,128)(2,1)S(1)}, bf16[2,128,384]{2,1,0:T(8,128)(2,1)S(1)}, u32[]{:S(2)}, u32[]{:S(2)}) %collective-permute-start) | collective-permute-done | bytes 196640 | tf_op jit(solution)/shard_map/ppermute | solution.py:499
  8.4 1.8 %collective-permute-done.1.refs_3_ = bf16[2,128,384]{2,1,0:T(8,128)(2,1)S(1)} collective-permute-done((bf16[2,128,384]{2,1,0:T(8,128)(2,1)S(1)}, bf16[2,128,384]{2,1,0:T(8,128)(2,1)S(1)}, u32[]{:S(2)}, u32[]{:S(2)}) %collective-permute-start.1) | collective-permute-done | bytes 196640 | tf_op jit(solution)/shard_map/ppermute | solution.py:500
  10.3 0.1 collective-permute-start.2
  10.4 5.5 %collective-permute-start.3 = (f32[4,384]{1,0:T(4,128)S(1)}, f32[4,384]{1,0:T(4,128)S(1)}, u32[]{:S(2)}, u32[]{:S(2)}) collective-permute-start(f32[4,384]{1,0:T(4,128)S(1)} %get-tuple-element.50), channel_id=1, source_target_pairs={{0,15},{1,2},{2,1},{3,4},{4,3},{5,6},{6,5},{7,8},{8,7},{9,10},{10,... | collective-permute-start | bytes 18440 | tf_op jit(solution)/shard_map/ppermute | solution.py:502
  15.9 1.9 %shard_map.223 = (bf16[512,384]{1,0:T(8,128)(2,1)S(1)}, bf16[512,1152]{1,0:T(8,128)(2,1)S(1)}, f32[8,384]{1,0:T(8,128)S(1)}) custom-call(bf16[2,128,384]{2,1,0:T(8,128)(2,1)S(1)} %get-tuple-element.81.refs_0_, bf16[2,128,384]{2,1,0:T(8,128)(2,1)S(1)} %get-tuple-element.80.refs_1_, bf16[2,128,384]{2,1,0:T(8,128)(2,1)S(1)} %collective-permute-done.refs_2_, ...), custom_call_target="tpu_custom_call" | custom-call | tf_op jit(solution)/shard_map/pallas_call | solution.py:176
  17.8 0.0 collective-permute-done.2.mate_ref
  17.8 0.0 collective-permute-done.3.far_ref
  17.8 3.6 %block_0.1 = (bf16[2,128,384]{2,1,0:T(8,128)(2,1)S(1)}, bf16[2,128,384]{2,1,0:T(8,128)(2,1)S(1)}) custom-call(f32[2,6]{1,0:T(2,128)S(1)} %get-tuple-element.42.scale_ref, bf16[512,384]{1,0:T(8,128)(2,1)S(1)} %get-tuple-element.46.mixed_ref, bf16[512,1152]{1,0:T(8,128)(2,1)S(1)} %get-tuple-element.47.units_ref, f32[8,384]{1,0:T(8,128)S(1)} %get-tuple-element.48.ends_ref, ...), custom_call_target="tpu_custom_call" | custom-call | tf_op jit(solution)/shard_map/block_0/pallas_call | solution.py:302
  21.4 3.2 %collective-permute-start.5 = (bf16[2,128,384]{2,1,0:T(8,128)(2,1)S(1)}, bf16[2,128,384]{2,1,0:T(8,128)(2,1)S(1)}, u32[]{:S(2)}, u32[]{:S(2)}) collective-permute-start(bf16[2,128,384]{2,1,0:T(8,128)(2,1)S(1)} %get-tuple-element.58.refs_0_), channel_id=1, source_target_pairs={{0,240},{16,0},{32,16},{48,32},{64,48},{80,64},{96,80},{112,96},{1... | collective-permute-start | bytes 589832 | tf_op jit(solution)/shard_map/ppermute | solution.py:500
  24.7 0.1 collective-permute-start.4
  24.7 2.4 %shard_map.221 = (bf16[2,2,128,128]{3,2,1,0:T(8,128)(2,1)S(1)}, bf16[384,128]{1,0:T(8,128)(2,1)S(1)}, f32[3,3,3,128]{3,2,1,0:T(4,128)S(1)}, bf16[3,128,128]{2,1,...) custom-call(bf16[2,2,128,128]{3,2,1,0:T(8,128)(2,1)} %refs_0_.2, ...), custom_call_target="tpu_custom_call" | custom-call | tf_op jit(solution)/shard_map/pallas_call | solution.py:547
  27.2 1.1 %collective-permute-done.5.refs_3_ = bf16[2,128,384]{2,1,0:T(8,128)(2,1)S(1)} collective-permute-done((bf16[2,128,384]{2,1,0:T(8,128)(2,1)S(1)}, bf16[2,128,384]{2,1,0:T(8,128)(2,1)S(1)}, u32[]{:S(2)}, u32[]{:S(2)}) %collective-permute-start.5) | collective-permute-done | bytes 196640 | tf_op jit(solution)/shard_map/ppermute | solution.py:500
  28.3 3.5 %collective-permute-done.4.refs_2_ = bf16[2,128,384]{2,1,0:T(8,128)(2,1)S(1)} collective-permute-done((bf16[2,128,384]{2,1,0:T(8,128)(2,1)S(1)}, bf16[2,128,384]{2,1,0:T(8,128)(2,1)S(1)}, u32[]{:S(2)}, u32[]{:S(2)}) %collective-permute-start.4) | collective-permute-done | bytes 196640 | tf_op jit(solution)/shard_map/ppermute | solution.py:499
  31.9 0.1 collective-permute-start.6
  32.0 4.8 %collective-permute-start.7 = (f32[4,384]{1,0:T(4,128)S(1)}, f32[4,384]{1,0:T(4,128)S(1)}, u32[]{:S(2)}, u32[]{:S(2)}) collective-permute-start(f32[4,384]{1,0:T(4,128)S(1)} %get-tuple-element.65), channel_id=1, source_target_pairs={{0,15},{1,2},{2,1},{3,4},{4,3},{5,6},{6,5},{7,8},{8,7},{9,10},{10,... | collective-permute-start | bytes 18440 | tf_op jit(solution)/shard_map/ppermute | solution.py:502
  36.8 1.9 %shard_map.225 = (bf16[512,384]{1,0:T(8,128)(2,1)S(1)}, bf16[512,1152]{1,0:T(8,128)(2,1)S(1)}, f32[8,384]{1,0:T(8,128)S(1)}) custom-call(bf16[2,128,384]{2,1,0:T(8,128)(2,1)S(1)} %get-tuple-element.58.refs_0_, bf16[2,128,384]{2,1,0:T(8,128)(2,1)S(1)} %get-tuple-element.59.refs_1_, bf16[2,128,384]{2,1,0:T(8,128)(2,1)S(1)} %collective-permute-done.4.refs_2_, ...), custom_call_target="tpu_custom_call" | custom-call | tf_op jit(solution)/shard_map/pallas_call | solution.py:176
  38.7 0.0 collective-permute-done.6.mate_ref
  38.7 0.2 collective-permute-done.7.far_ref
  38.9 3.7 %block_1.1 = (bf16[2,2,128,384]{3,2,1,0:T(8,128)(2,1)S(1)}, bf16[16,4,8,128]{3,2,1,0:T(8,128)(2,1)S(1)}) custom-call(f32[2,6]{1,0:T(2,128)S(1)} %get-tuple-element.42.scale_ref, bf16[512,384]{1,0:T(8,128)(2,1)S(1)} %get-tuple-element.61.mixed_ref, bf16[512,1152]{1,0:T(8,128)(2,1)S(1)} %get-tuple-element.62.units_ref, ...), custom_call_target="tpu_custom_call" | custom-call | tf_op jit(solution)/shard_map/block_1/pallas_call | solution.py:313
  42.6 15.6 %all_to_all.10.own_ref = bf16[16,4,8,128]{3,2,1,0:T(8,128)(2,1)S(1)} all-to-all(bf16[16,4,8,128]{3,2,1,0:T(8,128)(2,1)S(1)} %get-tuple-element.72.start_ref), channel_id=1, replica_groups=mesh['lat'=16,'lon'=8,'comp'=2] {'lat'}, dimensions={0} | all-to-all | bytes 262144 | tf_op jit(solution)/shard_map/all_to_all | solution.py:579
  58.3 0.7 collective-permute-start.9
  59.0 3.2 %collective-permute-start.8 = (bf16[16,4,8,128]{3,2,1,0:T(8,128)(2,1)S(1)}, bf16[16,4,8,128]{3,2,1,0:T(8,128)(2,1)S(1)}, u32[]{:S(2)}, u32[]{:S(2)}) collective-permute-start(bf16[16,4,8,128]{3,2,1,0:T(8,128)(2,1)S(1)} %all_to_all.10.own_ref), channel_id=1, source_target_pairs={{0,16},{1,17},{2,18},{3,19},{4,20},{5,21},{6,22},{7,23},{8,24},{9,... | collective-permute-start | bytes 393224 | tf_op jit(solution)/shard_map/ppermute | solution.py:581
  62.2 1.0 %collective-permute-done.9.next_ref = bf16[16,4,8,128]{3,2,1,0:T(8,128)(2,1)S(1)} collective-permute-done((bf16[16,4,8,128]{3,2,1,0:T(8,128)(2,1)S(1)}, bf16[16,4,8,128]{3,2,1,0:T(8,128)(2,1)S(1)}, u32[]{:S(2)}, u32[]{:S(2)}) %collective-permute-start.9) | collective-permute-done | bytes 131104 | tf_op jit(solution)/shard_map/ppermute | solution.py:582
  63.2 1.9 %collective-permute-done.8.pair_ref = bf16[16,4,8,128]{3,2,1,0:T(8,128)(2,1)S(1)} collective-permute-done((bf16[16,4,8,128]{3,2,1,0:T(8,128)(2,1)S(1)}, bf16[16,4,8,128]{3,2,1,0:T(8,128)(2,1)S(1)}, u32[]{:S(2)}, u32[]{:S(2)}) %collective-permute-start.8) | collective-permute-done | bytes 131104 | tf_op jit(solution)/shard_map/ppermute | solution.py:581
  65.1 1.8 %ocean.1 = bf16[16,4,8,128]{3,2,1,0:T(8,128)(2,1)S(1)} custom-call(f32[1,2]{1,0:T(1,128)S(1)} %get-tuple-element.41.refs_5_.scale_ref, bf16[16,4,8,128]{3,2,1,0:T(8,128)(2,1)S(1)} %all_to_all.10.own_ref, bf16[16,4,8,128]{3,2,1,0:T(8,128)(2,1)S(1)} %collective-permute-done.8.pair_ref, bf16[16,4,8,128]{3,2,1,0:T(8,128)(2,1)S(1)} %collective-permute-done.9.next_ref, ...), custom_call_target="tpu_custom_call" | custom-call | tf_op jit(solution)/shard_map/ocean/pallas_call | solution.py:407
  67.0 12.8 %all_to_all.11.last_ref = bf16[16,4,8,128]{3,2,1,0:T(8,128)(2,1)S(1)} all-to-all(bf16[16,4,8,128]{3,2,1,0:T(8,128)(2,1)S(1)} %ocean.1), channel_id=1, replica_groups=mesh['lat'=16,'lon'=8,'comp'=2] {'lat'}, dimensions={0} | all-to-all | bytes 262144 | tf_op jit(solution)/shard_map/all_to_all | solution.py:585
  79.8 1.1 %final.1 = (bf16[2,2,128,384]{3,2,1,0:T(8,128)(2,1)}, bf16[2,2,128,128]{3,2,1,0:T(8,128)(2,1)}) custom-call(bf16[16,4,8,128]{3,2,1,0:T(8,128)(2,1)S(1)} %all_to_all.11.last_ref, bf16[16,4,8,128]{3,2,1,0:T(8,128)(2,1)S(1)} %get-tuple-element.72.start_ref, bf16[2,2,128,384]{3,2,1,0:T(8,128)(2,1)S(1)} %get-tuple-element.78.cur_ref, ...), custom_call_target="tpu_custom_call" | custom-call | tf_op jit(solution)/shard_map/final/pallas_call | solution.py:454
  (2 shorter events, 0.1 us)
Async XLA Ops:
  1.7 6.7 %collective-permute-start = (bf16[2,128,384]{2,1,0:T(8,128)(2,1)S(1)}, bf16[2,128,384]{2,1,0:T(8,128)(2,1)S(1)}, u32[]{:S(2)}, u32[]{:S(2)}) collective-permute-start(bf16[2,128,384]{2,1,0:T(8,128)(2,1)S(1)} %get-tuple-element.80.refs_1_), channel_id=1, source_target_pairs={{0,16},{16,32},{32,48},{48,64},{64,80},{80,96},{96,112},{112,128},... | collective-permute-start | bytes 589832 | tf_op jit(solution)/shard_map/ppermute | solution.py:499
  3.7 6.5 %collective-permute-start.1 = (bf16[2,128,384]{2,1,0:T(8,128)(2,1)S(1)}, bf16[2,128,384]{2,1,0:T(8,128)(2,1)S(1)}, u32[]{:S(2)}, u32[]{:S(2)}) collective-permute-start(bf16[2,128,384]{2,1,0:T(8,128)(2,1)S(1)} %get-tuple-element.81.refs_0_), channel_id=1, source_target_pairs={{0,240},{16,0},{32,16},{48,32},{64,48},{80,64},{96,80},{112,96},{1... | collective-permute-start | bytes 589832 | tf_op jit(solution)/shard_map/ppermute | solution.py:500
  10.3 7.5 %collective-permute-start.2 = (f32[4,384]{1,0:T(4,128)S(1)}, f32[4,384]{1,0:T(4,128)S(1)}, u32[]{:S(2)}, u32[]{:S(2)}) collective-permute-start(f32[4,384]{1,0:T(4,128)S(1)} %get-tuple-element.49), channel_id=1, source_target_pairs={{0,1},{1,0},{2,3},{3,2},{4,5},{5,4},{6,7},{7,6},{8,9},{9,8},{10,11... | collective-permute-start | bytes 18440 | tf_op jit(solution)/shard_map/ppermute | solution.py:503
  10.4 7.4 %collective-permute-start.3 = (f32[4,384]{1,0:T(4,128)S(1)}, f32[4,384]{1,0:T(4,128)S(1)}, u32[]{:S(2)}, u32[]{:S(2)}) collective-permute-start(f32[4,384]{1,0:T(4,128)S(1)} %get-tuple-element.50), channel_id=1, source_target_pairs={{0,15},{1,2},{2,1},{3,4},{4,3},{5,6},{6,5},{7,8},{8,7},{9,10},{10,... | collective-permute-start | bytes 18440 | tf_op jit(solution)/shard_map/ppermute | solution.py:502
  21.4 6.9 %collective-permute-start.5 = (bf16[2,128,384]{2,1,0:T(8,128)(2,1)S(1)}, bf16[2,128,384]{2,1,0:T(8,128)(2,1)S(1)}, u32[]{:S(2)}, u32[]{:S(2)}) collective-permute-start(bf16[2,128,384]{2,1,0:T(8,128)(2,1)S(1)} %get-tuple-element.58.refs_0_), channel_id=1, source_target_pairs={{0,240},{16,0},{32,16},{48,32},{64,48},{80,64},{96,80},{112,96},{1... | collective-permute-start | bytes 589832 | tf_op jit(solution)/shard_map/ppermute | solution.py:500
  24.7 7.2 %collective-permute-start.4 = (bf16[2,128,384]{2,1,0:T(8,128)(2,1)S(1)}, bf16[2,128,384]{2,1,0:T(8,128)(2,1)S(1)}, u32[]{:S(2)}, u32[]{:S(2)}) collective-permute-start(bf16[2,128,384]{2,1,0:T(8,128)(2,1)S(1)} %get-tuple-element.59.refs_1_), channel_id=1, source_target_pairs={{0,16},{16,32},{32,48},{48,64},{64,80},{80,96},{96,112},{112,128},... | collective-permute-start | bytes 589832 | tf_op jit(solution)/shard_map/ppermute | solution.py:499
  31.9 6.8 %collective-permute-start.6 = (f32[4,384]{1,0:T(4,128)S(1)}, f32[4,384]{1,0:T(4,128)S(1)}, u32[]{:S(2)}, u32[]{:S(2)}) collective-permute-start(f32[4,384]{1,0:T(4,128)S(1)} %get-tuple-element.64), channel_id=1, source_target_pairs={{0,1},{1,0},{2,3},{3,2},{4,5},{5,4},{6,7},{7,6},{8,9},{9,8},{10,11... | collective-permute-start | bytes 18440 | tf_op jit(solution)/shard_map/ppermute | solution.py:503
  32.0 6.9 %collective-permute-start.7 = (f32[4,384]{1,0:T(4,128)S(1)}, f32[4,384]{1,0:T(4,128)S(1)}, u32[]{:S(2)}, u32[]{:S(2)}) collective-permute-start(f32[4,384]{1,0:T(4,128)S(1)} %get-tuple-element.65), channel_id=1, source_target_pairs={{0,15},{1,2},{2,1},{3,4},{4,3},{5,6},{6,5},{7,8},{8,7},{9,10},{10,... | collective-permute-start | bytes 18440 | tf_op jit(solution)/shard_map/ppermute | solution.py:502
  58.3 5.0 %collective-permute-start.9 = (bf16[16,4,8,128]{3,2,1,0:T(8,128)(2,1)S(1)}, bf16[16,4,8,128]{3,2,1,0:T(8,128)(2,1)S(1)}, u32[]{:S(2)}, u32[]{:S(2)}) collective-permute-start(bf16[16,4,8,128]{3,2,1,0:T(8,128)(2,1)S(1)} %all_to_all.10.own_ref), channel_id=1, source_target_pairs={{0,15},{1,2},{2,1},{3,4},{4,3},{5,6},{6,5},{7,8},{8,7},{9,10},{10,... | collective-permute-start | bytes 393224 | tf_op jit(solution)/shard_map/ppermute | solution.py:582
  59.0 6.2 %collective-permute-start.8 = (bf16[16,4,8,128]{3,2,1,0:T(8,128)(2,1)S(1)}, bf16[16,4,8,128]{3,2,1,0:T(8,128)(2,1)S(1)}, u32[]{:S(2)}, u32[]{:S(2)}) collective-permute-start(bf16[16,4,8,128]{3,2,1,0:T(8,128)(2,1)S(1)} %all_to_all.10.own_ref), channel_id=1, source_target_pairs={{0,16},{1,17},{2,18},{3,19},{4,20},{5,21},{6,22},{7,23},{8,24},{9,... | collective-permute-start | bytes 393224 | tf_op jit(solution)/shard_map/ppermute | solution.py:581
